TPU v7x, 32 devices: a whole 2x2x4 slice. The times are simulated.
32 devices in a mesh: ctx: 16 (over z, x, core), fsdp: 2 (over y).
Axes of the slice: x: 2, y: 2, z: 4, core: 2. Of those that a mesh axis runs over, the one named last changes fastest.
Arguments:
- tokens: bfloat16 [2, 4096, 512], P('fsdp', 'ctx'), may hold values from -6 to 6
- memory: bfloat16 [2, 2048, 512], P('fsdp', 'ctx'), may hold values from -6 to 6
- token_seg: int32 [2, 4096], P('fsdp'), may hold values from 0 to 7, as said below
- memory_seg: int32 [2, 2048], P('fsdp'), may hold values from 0 to 7, as said below
- out_grad: bfloat16 [2, 4096, 512], P('fsdp', 'ctx'), may hold values from -6 to 6
- in_proj: float32 [6, 512, 512], P(None, 'fsdp'), may hold values from -0.25 to 0.25
- out_proj: float32 [2, 512, 512], P(None, 'fsdp'), may hold values from -1 to 1
- ffn_in: float32 [512, 2048], P('fsdp'), may hold values from -0.25 to 0.25
- ffn_out: float32 [2048, 512], P('fsdp'), may hold values from -0.125 to 0.125
- norm_gain: float32 [3, 512], P(None, 'fsdp'), may hold values from 0.5 to 1.5
- bias_rows: float32 [10, 512], P(None, 'fsdp'), may hold values from -1.8 to 1.8
- ffn_bias: float32 [2048], P('fsdp'), may hold values from -3 to 3
Outputs:
- layer_out: float32 [2, 4096, 512], P('fsdp', 'ctx')
- tokens_grad: float32 [2, 4096, 512], P('fsdp', 'ctx')
- memory_grad: float32 [2, 2048, 512], P('fsdp', 'ctx')
- in_proj_grad: float32 [6, 512, 512], P(None, 'fsdp')
- out_proj_grad: float32 [2, 512, 512], P(None, 'fsdp')
- ffn_in_grad: float32 [512, 2048], P('fsdp')
- ffn_out_grad: float32 [2048, 512], P('fsdp')
- norm_gain_grad: float32 [3, 512], P(None, 'fsdp')
- bias_rows_grad: float32 [10, 512], P(None, 'fsdp')
- ffn_bias_grad: float32 [2048], P('fsdp')
Inputs may be any that keep to these rules, and one draw needn't show every extreme that they name: `token_seg`: along a sequence the ids never fall, and every document 0 to 7 occurs. In each sequence one document holds target tokens on every index of ctx. `memory_seg`: along a sequence the ids never fall; every document 0 to 7 has between 1 and 512 memory tokens, and the document that holds target tokens on every index of ctx has exactly 512.
All inputs are finite; a program needn't handle non-finite values.
Results may differ from a plain program's by a relative error of at most 0.022.
Values may be sent and summed in bfloat16 or wider, within the bound.
No kernel may reach another device: no remote copies, remote signals or barrier semaphores. Data moves between devices by JAX's collectives and lax.ppermute only.
A program may use at most 192 MiB of HBM per device.

v0:
```python
import math

import jax
import jax.numpy as jnp
from jax import lax
from jax.experimental import pallas as pl
from jax.experimental.pallas import tpu as pltpu
from jax.sharding import PartitionSpec as P

HEADS = 8
PAIRS = HEADS // 2
neg_fill = -1e30
eps_norm = 1e-05
self_block = 512
bf16 = jnp.bfloat16
f32 = jnp.float32
vmem_bytes = 60 * 1024 * 1024
half_rows = 256
chunk_rows = 32


def dot_nn(first_op, second_op):
    return jnp.dot(first_op, second_op, preferred_element_type=f32)


def dot_nt(first_op, second_op):
    return lax.dot_general(
        first_op, second_op, (((1,), (1,)), ((), ())), preferred_element_type=f32
    )


def dot_tn(first_op, second_op):
    return lax.dot_general(
        first_op, second_op, (((0,), (0,)), ((), ())), preferred_element_type=f32
    )


def stack_heads(tile):
    lane = lax.broadcasted_iota(jnp.int32, tile.shape, 1)
    half = tile.shape[1] // 2
    zero = jnp.zeros_like(tile)
    return jnp.concatenate(
        [jnp.where(lane < half, tile, zero), jnp.where(lane >= half, tile, zero)], axis=0
    )


def merge_heads(stacked):
    rows = stacked.shape[0] // 2
    lane = lax.broadcasted_iota(jnp.int32, (rows, stacked.shape[1]), 1)
    return jnp.where(lane < stacked.shape[1] // 2, stacked[:rows], stacked[rows:])


def tile_of(value, pair, tile_width):
    return value[:, pair * tile_width : (pair + 1) * tile_width]


def head_sums(product):
    width = product.shape[1]
    head = lax.broadcasted_iota(jnp.int32, (HEADS, width), 0)
    lane = lax.broadcasted_iota(jnp.int32, (HEADS, width), 1)
    pick = (lane // (width // HEADS) == head).astype(f32)
    return lax.dot_general(
        pick,
        product,
        (((1,), (1,)), ((), ())),
        precision=lax.Precision.HIGHEST,
        preferred_element_type=f32,
    )


def over_range(first, last):
    def run(step):
        def visit(index, carry):
            step(index, index)
            return carry

        lax.fori_loop(first, last, visit, 0)

    return run


def over_planes(info, plane_first, plane_count, first, last):
    def run(step):
        def visit(stored, carry):
            index = 2 * (info.plane ^ (plane_first + (stored >> 1))) + (stored & 1)

            @pl.when((index >= first) & (index < last))
            def _():
                step(stored, index)

            return carry

        lax.fori_loop(0, 2 * plane_count, visit, 0)

    return run


class RowInfo:
    def __init__(self, info_ref):
        self.table = info_ref
        self.half = info_ref.shape[1] // 2
        self.me = info_ref[5, 0]
        self.side = info_ref[6, 0]
        self.plane = self.me >> 2

    def ends(self, block):
        return block * self.half, (block + 1) * self.half - 1

    def self_keys(self, block):
        start, stop = self.ends(block)
        return self.table[0, start] // self_block, self.table[1, stop] // self_block + 1

    def cross_keys(self, block, size):
        start, stop = self.ends(block)
        return self.table[2, start] // size, self.table[3, stop] // size + 1

    def queries(self, block):
        start, stop = self.ends(block)
        return self.table[1, start] // self_block, self.table[4, stop] // self_block + 1


def twice(column):
    return jnp.concatenate([column, column], axis=0)


def stacked_tiles(rows):
    tile_width = rows.shape[1] // PAIRS
    return [stack_heads(tile_of(rows, pair, tile_width)) for pair in range(PAIRS)]


def attend_plain(q_block, kv_ref, low_col, high_col, run, key_rows, factor, acc_ref):
    width = q_block.shape[1]
    tile_width = width // PAIRS
    stacked = stacked_tiles(q_block)
    low2, high2 = twice(low_col), twice(high_col)
    ones = jnp.ones((key_rows, tile_width), bf16)

    def step(stored, index):
        base = pl.multiple_of(stored * key_rows, key_rows)
        key_pos = index * key_rows + lax.broadcasted_iota(jnp.int32, (1, key_rows), 1)
        allowed = (key_pos >= low2) & (key_pos <= high2)
        for pair in range(PAIRS):
            start = pair * tile_width
            keys = kv_ref[pl.ds(base, key_rows), start : start + tile_width]
            values = kv_ref[pl.ds(base, key_rows), width + start : width + start + tile_width]
            scores = dot_nt(stacked[pair], keys)
            weights = jnp.where(allowed, jnp.exp2(scores * factor), 0.0).astype(bf16)
            acc_ref[pair] += dot_nn(weights, jnp.concatenate([values, ones], axis=1))

    run(step)


def weighted_rows(acc_ref):
    tile_width = acc_ref.shape[2] // 2
    tops = [merge_heads(acc_ref[pair, :, 0:tile_width]) for pair in range(PAIRS)]
    sums = [merge_heads(acc_ref[pair, :, tile_width:]) for pair in range(PAIRS)]
    return jnp.concatenate(tops, axis=1), jnp.concatenate(sums, axis=1)


def in_range(sums):
    return (jnp.min(sums) > 2.0**-100) & (jnp.max(sums) < 2.0**100)


def attend_running(q_block, parts, low_col, high_col, key_rows, factor, scratch):
    max_ref, sum_ref, acc_ref = scratch
    width = q_block.shape[1]
    tile_width = width // PAIRS
    stacked = stacked_tiles(q_block)
    low2, high2 = twice(low_col), twice(high_col)
    max_ref[...] = jnp.full(max_ref.shape, neg_fill, f32)
    sum_ref[...] = jnp.zeros(sum_ref.shape, f32)
    acc_ref[...] = jnp.zeros(acc_ref.shape, f32)
    for kv_ref, run in parts:

        def step(stored, index, kv_ref=kv_ref):
            base = pl.multiple_of(stored * key_rows, key_rows)
            key_pos = index * key_rows + lax.broadcasted_iota(jnp.int32, (1, key_rows), 1)
            allowed = (key_pos >= low2) & (key_pos <= high2)
            for pair in range(PAIRS):
                start = pair * tile_width
                keys = kv_ref[pl.ds(base, key_rows), start : start + tile_width]
                values = kv_ref[pl.ds(base, key_rows), width + start : width + start + tile_width]
                scores = jnp.where(allowed, dot_nt(stacked[pair], keys), neg_fill)
                old_max = max_ref[pair]
                new_max = jnp.maximum(old_max, jnp.max(scores, axis=1, keepdims=True))
                probs = jnp.exp2((scores - new_max) * factor)
                rescale = jnp.exp2((old_max - new_max) * factor)
                sum_ref[pair] = sum_ref[pair] * rescale + jnp.sum(probs, axis=1, keepdims=True)
                acc_ref[pair] = acc_ref[pair] * rescale + dot_nn(probs.astype(bf16), values)
                max_ref[pair] = new_max

        run(step)
    outputs, logs = [], []
    for pair in range(PAIRS):
        outputs.append(merge_heads(acc_ref[pair] / sum_ref[pair]))
        column = max_ref[pair] * factor + jnp.log2(sum_ref[pair])
        logs.append(merge_heads(jnp.broadcast_to(column, acc_ref.shape[1:])))
    return jnp.concatenate(outputs, axis=1), jnp.concatenate(logs, axis=1)


def log_rows_of(lane_logs):
    return head_sums(lane_logs) * (HEADS / lane_logs.shape[1])


def query_grads(
    q_block, g_block, kv_ref, low_col, high_col, log_ref, delta_ref, run, key_rows, factor, acc_ref
):
    width = q_block.shape[1]
    tile_width = width // PAIRS
    q2, g2 = stacked_tiles(q_block), stacked_tiles(g_block)
    low2, high2 = twice(low_col), twice(high_col)

    def step(stored, index):
        base = pl.multiple_of(stored * key_rows, key_rows)
        key_pos = index * key_rows + lax.broadcasted_iota(jnp.int32, (1, key_rows), 1)
        allowed = (key_pos >= low2) & (key_pos <= high2)
        for pair in range(PAIRS):
            start = pair * tile_width
            keys = kv_ref[pl.ds(base, key_rows), start : start + tile_width]
            values = kv_ref[pl.ds(base, key_rows), width + start : width + start + tile_width]
            scores = dot_nt(q2[pair], keys)
            repeats = key_rows // log_ref.shape[2]
            logs = jnp.concatenate([log_ref[pair]] * repeats, axis=1)
            deltas = jnp.concatenate([delta_ref[pair]] * repeats, axis=1)
            probs = jnp.where(allowed, jnp.exp2(scores * factor - logs), 0.0)
            prob_grad = dot_nt(g2[pair], values)
            score_grad = (probs * (prob_grad - deltas)).astype(bf16)
            acc_ref[pair] += dot_nn(score_grad, keys)

    run(step)


def key_grads(k_block, v_block, q_ref, g_ref, stats_ref, low_col, high_col, run, factor, dk_ref, dv_ref):
    width = k_block.shape[1]
    tile_width = width // PAIRS
    rows = k_block.shape[0]
    query_rows = self_block
    blocks = query_rows // rows
    k2, v2 = stacked_tiles(k_block), stacked_tiles(v_block)
    low2, high2 = twice(low_col), twice(high_col)

    def step(stored, index):
        base = pl.multiple_of(stored * query_rows, query_rows)
        q_base = pl.multiple_of(index * query_rows, query_rows)
        query_pos = q_base + lax.broadcasted_iota(jnp.int32, (1, query_rows), 1)
        allowed = (query_pos >= low2) & (query_pos <= high2)
        stats = jnp.concatenate([stats_ref[stored * blocks + u] for u in range(blocks)], axis=1)

        def two_rows(first_row):
            return jnp.concatenate(
                [
                    jnp.broadcast_to(stats[first_row : first_row + 1], (rows, query_rows)),
                    jnp.broadcast_to(stats[first_row + 1 : first_row + 2], (rows, query_rows)),
                ],
                axis=0,
            )

        for pair in range(PAIRS):
            lanes = slice(pair * tile_width, (pair + 1) * tile_width)
            queries = q_ref[pl.ds(q_base, query_rows), lanes]
            upstream = g_ref[pl.ds(base, query_rows), lanes]
            scores = dot_nt(k2[pair], queries)
            probs = jnp.where(allowed, jnp.exp2(scores * factor - two_rows(2 * pair)), 0.0)
            prob_grad = dot_nt(v2[pair], upstream)
            score_grad = (probs * (prob_grad - two_rows(HEADS + 2 * pair))).astype(bf16)
            dk_ref[pair] += dot_nn(score_grad, queries)
            dv_ref[pair] += dot_nn(probs.astype(bf16), upstream)

    run(step)


def merged_rows(acc_ref):
    return jnp.concatenate([merge_heads(acc_ref[pair]) for pair in range(PAIRS)], axis=1)


def chunk_views(piece_refs, planes):
    for s in range(planes):
        for bits in range(4):
            yield s, bits, piece_refs[(bits >> 1) + 2 * (bits & 1)].at[s]


def fill_rows(target, parts, info, skip=0, lead=0):
    own, fetched, other = parts
    rows = own.shape[-2]
    core = info.me & 1
    starts = (
        info.side * rows,
        (1 - info.side) * rows + core * (rows // 2),
        (1 - info.side) * rows + (1 - core) * (rows // 2),
    )
    for number, (part, start) in enumerate(zip((own, fetched, other), starts)):
        size = rows // 2 if number else rows
        at = pl.ds(pl.multiple_of(start, rows // 2), size)
        if len(target.shape) == 3:
            for k in range(target.shape[0]):
                first = skip + k * size
                window = part[first : first + size] if number else part[lead + k]
                target[k, at, :] = window.astype(bf16)
        elif target.shape[1] == part.shape[1]:
            target[at, :] = (part[skip : skip + size] if number else part[...]).astype(bf16)
        elif not number:
            target[at, :] = part[...].astype(bf16)
        else:
            width = part.shape[1]
            for k in range(target.shape[1] // width):
                first = skip + k * size
                target[at, k * width : (k + 1) * width] = part[first : first + size]


def attend_back(
    q_block, g_block, kv_ref, dkv_ref, low_row, high_row, log_rows, delta_rows,
    first, last, key_rows, factor, scale, dq_ref, adding,
):
    width = q_block.shape[1]
    tile_width = width // PAIRS
    rows = q_block.shape[0]
    q2 = [stack_heads(tile_of(q_block, pair, tile_width)) for pair in range(PAIRS)]
    g2 = [stack_heads(tile_of(g_block, pair, tile_width)) for pair in range(PAIRS)]
    low2 = jnp.concatenate([low_row, low_row], axis=1)
    high2 = jnp.concatenate([high_row, high_row], axis=1)
    dq_ref[...] = jnp.zeros(dq_ref.shape, f32)

    def step(index, carry):
        base = pl.multiple_of(index * key_rows, key_rows)
        key_pos = base + lax.broadcasted_iota(jnp.int32, (key_rows, 1), 0)
        allowed = (key_pos >= low2) & (key_pos <= high2)
        for pair in range(PAIRS):
            key_at = (pl.ds(base, key_rows), slice(pair * tile_width, (pair + 1) * tile_width))
            value_at = (
                pl.ds(base, key_rows),
                slice(width + pair * tile_width, width + (pair + 1) * tile_width),
            )
            keys = kv_ref[key_at]
            values = kv_ref[value_at]
            scores = dot_nt(keys, q2[pair])
            probs = jnp.where(allowed, jnp.exp2(scores * factor - log_rows[pair]), 0.0)
            prob_grad = dot_nt(values, g2[pair])
            score_grad = (probs * (prob_grad - delta_rows[pair])).astype(bf16)
            key_grad = dot_nn(score_grad, q2[pair]) * scale
            value_grad = dot_nn(probs.astype(bf16), g2[pair])
            if adding:
                key_grad = key_grad + dkv_ref[key_at].astype(f32)
                value_grad = value_grad + dkv_ref[value_at].astype(f32)
            dkv_ref[key_at] = key_grad.astype(bf16)
            dkv_ref[value_at] = value_grad.astype(bf16)
            dq_ref[pair] += dot_tn(keys, score_grad)
        return carry

    lax.fori_loop(first, last, step, 0)
    tiles = []
    for pair in range(PAIRS):
        both = dq_ref[pair]
        feature = lax.broadcasted_iota(jnp.int32, (tile_width, rows), 0)
        picked = jnp.where(feature < tile_width // 2, both[:, :rows], both[:, rows:])
        tiles.append(jnp.transpose(picked) * scale)
    return jnp.concatenate(tiles, axis=1)


def split_three(value):
    one = value.astype(bf16)
    rest = value - one.astype(f32)
    two = rest.astype(bf16)
    three = (rest - two.astype(f32)).astype(bf16)
    return [one, two, three]


def side_by_side(stats):
    rows = stats.shape[0] // 2
    return jnp.concatenate([stats[:rows], stats[rows:]], axis=1)


class PieceSink:
    def __init__(self, keep_ref, send_ref, scratch_ref, me, side):
        self.keep, self.send, self.scratch, self.me, self.side = keep_ref, send_ref, scratch_ref, me, side

    def emit(self, block, stride, offset):
        planes = self.keep.shape[2]
        piece = half_rows // (4 * planes)
        at = slice(block * piece, (block + 1) * piece)
        for s in range(planes):
            for bits in range(4):
                dc, dx = bits & 1, bits >> 1
                owner = self.me ^ (4 * s + bits)
                for fy in range(2):
                    source = (self.side ^ fy) * stride + offset + owner * piece
                    rows = self.scratch[pl.ds(pl.multiple_of(source, piece), piece), :]
                    target = self.send if dc else self.keep
                    target[fy, dx, s, at, :] = rows.astype(bf16)

    def put(self, block, matrix):
        rows = matrix.shape[0]
        self.scratch[0:rows, :] = matrix.astype(f32)
        blocks = rows // (2 * half_rows)
        for b in range(blocks):
            self.emit(block + b, rows // 2, b * half_rows)


class PlainSink:
    def __init__(self, plain_ref):
        self.plain = plain_ref

    def put(self, block, matrix):
        size = 2 * half_rows
        for b in range(matrix.shape[0] // size):
            self.plain[block + b] = matrix[b * size : (b + 1) * size].astype(bf16)


def pair_rows(by_head, block, rows, pair):
    at = slice(block * rows, (block + 1) * rows)
    return jnp.concatenate(
        [by_head[2 * pair : 2 * pair + 1, at], by_head[2 * pair + 1 : 2 * pair + 2, at]], axis=1
    )


def norm_stats(residual):
    centre = residual - jnp.mean(residual, axis=1, keepdims=True)
    spread = jnp.mean(centre * centre, axis=1, keepdims=True)
    inverse = lax.rsqrt(spread + eps_norm)
    return centre * inverse, inverse


def norm_back(normed, inverse, gain_row, upstream):
    scaled = upstream * gain_row
    mean_one = jnp.mean(scaled, axis=1, keepdims=True)
    mean_two = jnp.mean(scaled * normed, axis=1, keepdims=True)
    return (scaled - mean_one - normed * mean_two) * inverse


def column_sum(matrix):
    return jnp.sum(matrix.astype(f32), axis=0, keepdims=True)


def project_chunks(pieces, planes, kv_ref, w_ref, shift, info):
    width = w_ref.shape[2]
    rows = pieces[0].shape[1]
    for s, bits, chunk in chunk_views(pieces, planes):
        start = 4 * rows * s + rows * ((info.me & 3) ^ bits)
        at = pl.ds(pl.multiple_of(start, rows), rows)
        block = chunk[...]
        kv_ref[at, 0:width] = dot_nn(block, w_ref[1]).astype(bf16)
        kv_ref[at, width:] = (dot_nn(block, w_ref[2]) + shift).astype(bf16)


def first_forward_kernel(info_ref, x_ref, bias_ref, cols_ref, *refs, factor, planes, shards):
    maps, refs = refs[:shards], refs[shards:]
    pieces, refs = refs[:4], refs[4:]
    q_ref, kv_rows_ref, kv_ref, w_ref, top_ref, sums_ref, acc_ref = refs
    info = RowInfo(info_ref)
    width = x_ref.shape[1]
    half = info.half
    if shards == 1:
        w_ref[...] = maps[0][0:3]
    else:
        fill_rows(w_ref, maps, info)
    shift = bias_ref[1:2, :]
    project_chunks(pieces, planes, kv_ref, w_ref, shift, info)
    x_rows = x_ref[...]
    q_rows = (dot_nn(x_rows, w_ref[0]) + bias_ref[0:1, :]).astype(bf16)
    q_ref[...] = q_rows
    kv_rows_ref[:, 0:width] = dot_nn(x_rows, w_ref[1]).astype(bf16)
    kv_rows_ref[:, width:] = (dot_nn(x_rows, w_ref[2]) + shift).astype(bf16)
    for block in range(2):
        at = slice(block * half, (block + 1) * half)
        acc_ref[...] = jnp.zeros(acc_ref.shape, f32)
        run = over_planes(info, 0, planes, *info.self_keys(block))
        attend_plain(
            q_rows[at], kv_ref, cols_ref[at, 0:1], cols_ref[at, 1:2], run, self_block, factor, acc_ref
        )
        top_ref[at, :], sums_ref[at, :] = weighted_rows(acc_ref)


def second_forward_kernel(
    info_ref, kv_near_ref, q_in_ref, bias_ref, cols_ref, w_ref, top_ref, sums_ref, *refs,
    factor, planes,
):
    pieces, refs = refs[:4], refs[4:]
    a_ref, log_ref, kv_ref, acc_ref, max_ref, sum_ref, run_ref, lane_ref, near_ref, near_sem = refs
    info = RowInfo(info_ref)
    half = info.half
    project_chunks(pieces, planes, kv_ref, w_ref, bias_ref[1:2, :], info)
    fine = None
    for block in range(2):
        at = slice(block * half, (block + 1) * half)
        acc_ref[...] = jnp.zeros(acc_ref.shape, f32)
        run = over_planes(info, planes, planes, *info.self_keys(block))
        attend_plain(
            q_in_ref[at, :], kv_ref, cols_ref[at, 0:1], cols_ref[at, 1:2], run, self_block, factor,
            acc_ref,
        )
        top, sums = weighted_rows(acc_ref)
        sums = sums + sums_ref[at, :]
        a_ref[at, :] = (top + top_ref[at, :]) / sums
        lane_ref[at, :] = jnp.log2(sums)
        fine = in_range(sums) if fine is None else fine & in_range(sums)

    @pl.when(jnp.logical_not(fine))
    def _():
        copy = pltpu.make_async_copy(kv_near_ref, near_ref, near_sem)
        copy.start()
        copy.wait()
        for block in range(2):
            at = slice(block * half, (block + 1) * half)
            keys = info.self_keys(block)
            a_ref[at, :], lane_ref[at, :] = attend_running(
                q_in_ref[at, :],
                [
                    (near_ref, over_planes(info, 0, planes, *keys)),
                    (kv_ref, over_planes(info, planes, planes, *keys)),
                ],
                cols_ref[at, 0:1], cols_ref[at, 1:2], self_block, factor, (max_ref, sum_ref, run_ref),
            )

    log_ref[...] = log_rows_of(lane_ref[...])


def project_kernel(info_ref, w_ref, bias_ref, *refs, planes):
    pieces, (q_ref,) = refs[:8], refs[8:]
    info = RowInfo(info_ref)
    for part in range(2):
        for s, bits, chunk in chunk_views(pieces[4 * part : 4 * part + 4], planes):
            rows = chunk.shape[0]
            place = info.me ^ (4 * (part * planes + s) + bits)
            at = pl.ds(pl.multiple_of(place * rows, rows), rows)
            q_ref[at, :] = (dot_nn(chunk[...], w_ref[0]) + bias_ref[0:1, :]).astype(bf16)


def middle_forward_kernel(
    info_ref, x_ref, a_ref, g_ref, cols_ref, gain_ref, bias_ref, ffn_bias_ref, mem_ref, *refs,
    factor, shards, cross_rows,
):
    late, refs = (refs[:3], refs[3:]) if shards == 1 else (refs[:5], refs[5:])
    (
        out_ref, a_low_ref, h1_ref, h2_ref, f_ref, e3_ref, gu_ref, e2_ref, ac_ref, gr2_ref, r1_ref,
        qc_ref, cross_ref, cross_log_ref, kvc_ref, sums_ref, csum_ref, wc_ref,
        acc_ref, max_ref, sum_ref, run_ref, lane_ref, *whole_refs,
    ) = refs
    info = RowInfo(info_ref)
    if shards == 1:
        maps_ref, u_ref, v_ref = late
        wc_ref[...] = maps_ref[3:8]
    else:
        maps_ref, up_ref, down_ref, one, two = late
        u_ref, v_ref = whole_refs
        size = maps_ref.shape[1] // 2
        fill_rows(wc_ref, (maps_ref, one, two), info, 0, 3)
        fill_rows(v_ref, (down_ref, one, two), info, 5 * size)
        fill_rows(u_ref, (up_ref, one, two), info, 5 * size + down_ref.shape[0] // 2)
    rows, width = x_ref.shape
    half = rows // 2
    cross_block = cross_rows
    cross_range = [info.cross_keys(block, cross_block) for block in range(2)]
    live_first = jnp.minimum(cross_range[0][0], cross_range[1][0])
    live_last = jnp.maximum(cross_range[0][1], cross_range[1][1])

    def project(index, carry):
        at = pl.ds(pl.multiple_of(index * cross_block, cross_block), cross_block)
        block = mem_ref[at, :]
        kvc_ref[at, 0:width] = dot_nn(block, wc_ref[1]).astype(bf16)
        kvc_ref[at, width:] = (dot_nn(block, wc_ref[2]) + bias_ref[5:6, :]).astype(bf16)
        return carry

    lax.fori_loop(live_first, live_last, project, 0)
    attn_self = a_ref[...]
    a_low = attn_self.astype(bf16)
    a_low_ref[...] = a_low
    r1 = x_ref[...].astype(f32) + (dot_nn(a_low, wc_ref[3]) + bias_ref[2:3, :])
    r1_ref[...] = r1
    n1, inv1 = norm_stats(r1)
    h1 = n1 * gain_ref[0:1, :] + bias_ref[3:4, :]
    h1_low = h1.astype(bf16)
    h1_ref[...] = h1_low
    qc = (dot_nn(h1_low, wc_ref[0]) + bias_ref[4:5, :]).astype(bf16)
    qc_ref[...] = qc
    fine = None
    for block in range(2):
        at = slice(block * half, (block + 1) * half)
        acc_ref[...] = jnp.zeros(acc_ref.shape, f32)
        attend_plain(
            qc[at], kvc_ref, cols_ref[at, 2:3], cols_ref[at, 3:4], over_range(*cross_range[block]),
            cross_block, factor, acc_ref,
        )
        top, weights = weighted_rows(acc_ref)
        cross_ref[at, :] = top / weights
        lane_ref[at, :] = jnp.log2(weights)
        fine = in_range(weights) if fine is None else fine & in_range(weights)

    @pl.when(jnp.logical_not(fine))
    def _():
        for block in range(2):
            at = slice(block * half, (block + 1) * half)
            cross_ref[at, :], lane_ref[at, :] = attend_running(
                qc_ref[at, :], [(kvc_ref, over_range(*cross_range[block]))],
                cols_ref[at, 2:3], cols_ref[at, 3:4], cross_block, factor, (max_ref, sum_ref, run_ref),
            )

    cross_log_ref[...] = log_rows_of(lane_ref[...])
    attn_cross = cross_ref[...]
    ac_low = attn_cross.astype(bf16)
    ac_ref[...] = ac_low
    r2 = h1 + (dot_nn(ac_low, wc_ref[4]) + bias_ref[6:7, :])
    n2, inv2 = norm_stats(r2)
    h2 = n2 * gain_ref[1:2, :] + bias_ref[7:8, :]
    h2_low = h2.astype(bf16)
    h2_ref[...] = h2_low
    u = dot_nn(h2_low, u_ref[...]) + ffn_bias_ref[...]
    sig = 1.0 / (1.0 + jnp.exp(-u))
    act = (u / (1.0 + jnp.exp(-u))).astype(bf16)
    f_ref[...] = act
    slope = sig * (1.0 + u * (1.0 - sig))
    r3 = h2 + (dot_nn(act, v_ref[...]) + bias_ref[8:9, :])
    n3, inv3 = norm_stats(r3)
    out_ref[...] = n3 * gain_ref[2:3, :] + bias_ref[9:10, :]
    sums_ref[...] = jnp.zeros_like(sums_ref)
    upstream = g_ref[...].astype(f32)
    sums_ref[2:3, :] = column_sum(upstream * n3)
    sums_ref[12:13, :] = column_sum(upstream)
    gr3 = norm_back(n3, inv3, gain_ref[2:3, :], upstream)
    e3 = gr3.astype(bf16)
    e3_ref[...] = e3
    sums_ref[11:12, :] = column_sum(e3)
    gu = (dot_nt(e3, v_ref[...]) * slope).astype(bf16)
    gu_ref[...] = gu
    csum_ref[...] = column_sum(gu)
    gh2 = gr3 + dot_nt(gu, u_ref[...])
    sums_ref[1:2, :] = column_sum(gh2 * n2)
    sums_ref[10:11, :] = column_sum(gh2)
    gr2 = norm_back(n2, inv2, gain_ref[1:2, :], gh2)
    gr2_ref[...] = gr2
    e2 = gr2.astype(bf16)
    e2_ref[...] = e2
    sums_ref[9:10, :] = column_sum(e2)


def middle_backward_kernel(
    info_ref, a_ref, log_ref, rows_ref, gain_ref, wc_ref, e2_ref, gr2_ref, r1_ref, qc_ref,
    cross_ref, cross_log_ref, kvc_ref, sums_in_ref,
    e1_ref, dqc_ref, ga_ref, gr1_ref, delta_ref, dkvc_ref, sums_ref, dq_ref,
    *, factor, scale, cross_rows,
):
    info = RowInfo(info_ref)
    rows, width = a_ref.shape
    half = rows // 2
    cross_block = cross_rows
    cross_range = [info.cross_keys(block, cross_block) for block in range(2)]
    live_first = jnp.minimum(cross_range[0][0], cross_range[1][0])
    live_last = jnp.maximum(cross_range[0][1], cross_range[1][1])
    sums_ref[...] = sums_in_ref[...]
    n1, inv1 = norm_stats(r1_ref[...])
    attn_self, attn_cross = a_ref[...], cross_ref[...]
    gr2, e2, qc, cross_logs = gr2_ref[...], e2_ref[...], qc_ref[...], cross_log_ref[...]

    def clear(index, carry):
        at = pl.ds(pl.multiple_of(index * cross_block, cross_block), cross_block)
        dkvc_ref[at, :] = jnp.zeros((cross_block, 2 * width), bf16)
        return carry

    lax.fori_loop(live_first, live_last, clear, 0)
    gac = dot_nt(e2, wc_ref[4]).astype(bf16)
    sums_ref[8:9, :] = column_sum(gac)
    delta_cross = head_sums(gac.astype(f32) * attn_cross)
    grads = []
    for block in (1, 0):
        at = slice(block * half, (block + 1) * half)
        grads.append(
            attend_back(
                qc[at], gac[at], kvc_ref, dkvc_ref, rows_ref[2:3, at], rows_ref[3:4, at],
                [pair_rows(cross_logs, block, half, p) for p in range(PAIRS)],
                [pair_rows(delta_cross, block, half, p) for p in range(PAIRS)],
                *cross_range[block], cross_block, factor, scale,
                dq_ref, True,
            )
        )
    dqc = jnp.concatenate([grads[1], grads[0]], axis=0).astype(bf16)
    dqc_ref[...] = dqc
    sums_ref[7:8, :] = column_sum(dqc)
    gh1 = gr2 + dot_nt(dqc, wc_ref[0])
    sums_ref[0:1, :] = column_sum(gh1 * n1)
    sums_ref[6:7, :] = column_sum(gh1)
    gr1 = norm_back(n1, inv1, gain_ref[0:1, :], gh1)
    gr1_ref[...] = gr1
    e1 = gr1.astype(bf16)
    e1_ref[...] = e1
    sums_ref[5:6, :] = column_sum(e1)
    ga = dot_nt(e1, wc_ref[3]).astype(bf16)
    ga_ref[0:rows, :] = ga
    sums_ref[4:5, :] = column_sum(ga)
    delta = head_sums(ga.astype(f32) * attn_self)
    delta_ref[...] = delta
    extra = split_three(side_by_side(log_ref[...])) + split_three(side_by_side(delta))
    extra.append(jnp.zeros((2 * HEADS // 2, width), bf16))
    ga_ref[rows:, :] = jnp.concatenate([e.astype(f32) for e in extra], axis=0).astype(bf16)


def memory_grads_kernel(
    info_ref, mem_ref, wc_ref, dkvc_ref, pm_ref, dwc_ref, dw_acc_ref, *, cross_block
):
    info = RowInfo(info_ref)
    width = mem_ref.shape[1]
    cross_range = [info.cross_keys(block, cross_block) for block in range(2)]
    live_first = jnp.minimum(cross_range[0][0], cross_range[1][0])
    live_last = jnp.maximum(cross_range[0][1], cross_range[1][1])
    pm_ref[...] = jnp.zeros(pm_ref.shape, bf16)
    dw_acc_ref[...] = jnp.zeros(dw_acc_ref.shape, f32)

    def memory_step(index, carry):
        at = pl.ds(pl.multiple_of(index * cross_block, cross_block), cross_block)
        grads_block = dkvc_ref[at, :]
        block = dot_nt(grads_block[:, :width], wc_ref[1]) + dot_nt(grads_block[:, width:], wc_ref[2])
        pm_ref[at, :] = block.astype(bf16)
        dw_acc_ref[...] += dot_tn(mem_ref[at, :], grads_block)
        return carry

    lax.fori_loop(live_first, live_last, memory_step, 0)
    dwc_ref[...] = dw_acc_ref[...].astype(bf16)


def query_backward_kernel(
    info_ref, q_ref, ga_ref, kv_near_ref, kv_far_ref, log_ref, delta_ref, cols_ref, dq_ref, acc_ref,
    log_rep_ref, delta_rep_ref, *, factor, scale, planes,
):
    info = RowInfo(info_ref)
    rows = q_ref.shape[0]
    half = info.half
    pad = jnp.zeros((128 - 2 * HEADS, rows), f32)
    stat_cols = jnp.transpose(jnp.concatenate([log_ref[...], delta_ref[...], pad], axis=0))

    def stat_column(at, head):
        return jnp.concatenate(
            [stat_cols[at, head : head + 1], stat_cols[at, head + 1 : head + 2]], axis=0
        )

    for block in range(2):
        at = slice(block * half, (block + 1) * half)
        acc_ref[...] = jnp.zeros(acc_ref.shape, f32)
        for p in range(PAIRS):
            log_rep_ref[p] = jnp.broadcast_to(stat_column(at, 2 * p), log_rep_ref.shape[1:])
            delta_rep_ref[p] = jnp.broadcast_to(stat_column(at, HEADS + 2 * p), log_rep_ref.shape[1:])
        for part, kv_ref in enumerate((kv_near_ref, kv_far_ref)):
            query_grads(
                q_ref[at, :], ga_ref[at, :], kv_ref, cols_ref[at, 0:1], cols_ref[at, 1:2],
                log_rep_ref, delta_rep_ref,
                over_planes(info, part * planes, planes, *info.self_keys(block)),
                self_block, factor, acc_ref,
            )
        dq_ref[at, :] = (merged_rows(acc_ref) * scale).astype(bf16)


def key_backward_kernel(
    info_ref, kv_rows_ref, q_all_ref, cols_ref, *refs, factor, scale, planes, part, last,
    total_planes,
):
    state_in, refs = (refs[:2], refs[2:]) if part else ((), refs)
    pieces, refs = refs[:4], refs[4:]
    if last:
        dk_out_ref, dv_out_ref, g_ref, stats_ref, dk_ref, dv_ref = refs
    else:
        dk_ref, dv_ref, g_ref, stats_ref = refs
    info = RowInfo(info_ref)
    half = info.half
    rows = 2 * half
    width = q_all_ref.shape[1]
    for s, bits, chunk in chunk_views(pieces, planes):
        place = (info.me & 3) ^ bits
        extra = chunk[rows : rows + chunk_rows, :].astype(f32)
        logs = extra[0:4] + extra[4:8] + extra[8:12]
        deltas = extra[12:16] + extra[16:20] + extra[20:24]
        for side in range(2):
            block = 8 * s + 4 * side + (place if side == 0 else 3 - place)
            lanes = slice(side * half, (side + 1) * half)
            high = slice(rows + side * half, rows + (side + 1) * half)
            g_ref[pl.ds(pl.multiple_of(block * half, half), half), :] = chunk[lanes, :]
            stats_ref[block] = jnp.concatenate(
                [logs[:, lanes], logs[:, high], deltas[:, lanes], deltas[:, high]], axis=0
            )

    def groups(first, stop):
        def run(step):
            def visit(stored, carry):
                plane = info.plane ^ (part * planes + (stored >> 1))
                index = jnp.where((stored & 1) == 0, plane, 2 * total_planes - 1 - plane)

                @pl.when((index >= first) & (index < stop))
                def _():
                    step(stored, index)

                return carry

            lax.fori_loop(0, 2 * planes, visit, 0)

        return run

    for block in range(2):
        at = slice(block * half, (block + 1) * half)
        if part:
            dk_ref[block] = state_in[0][block]
            dv_ref[block] = state_in[1][block]
        else:
            dk_ref[block] = jnp.zeros(dk_ref.shape[1:], f32)
            dv_ref[block] = jnp.zeros(dv_ref.shape[1:], f32)
        key_grads(
            kv_rows_ref[at, 0:width], kv_rows_ref[at, width:], q_all_ref, g_ref, stats_ref,
            cols_ref[at, 1:2], cols_ref[at, 4:5], groups(*info.queries(block)), factor,
            dk_ref.at[block], dv_ref.at[block],
        )
    if not last:
        return
    dk = jnp.concatenate([merged_rows(dk_ref.at[b]) for b in range(2)], axis=0) * scale
    dv = jnp.concatenate([merged_rows(dv_ref.at[b]) for b in range(2)], axis=0)
    dk_out_ref[...] = dk.astype(bf16)
    dv_out_ref[...] = dv.astype(bf16)


def self_grads_kernel(
    info_ref, x_ref, gr1_ref, dq_ref, dk_ref, dv_ref, w_ref, tok_ref, *refs, plain
):
    sink_refs, (dw_ref,) = (refs[:1], refs[1:]) if plain else (refs[:2], refs[2:])
    info = RowInfo(info_ref)
    dk, dv = dk_ref[...], dv_ref[...]
    tok = gr1_ref[...] + dot_nt(dq_ref[...], w_ref[0]) + dot_nt(dk, w_ref[1]) + dot_nt(dv, w_ref[2])
    tok_ref[...] = tok.astype(bf16)
    sink = PlainSink(*sink_refs) if plain else PieceSink(*sink_refs, dw_ref, info.me, info.side)
    x_rows = x_ref[...]
    sink.put(0, dot_tn(x_rows, dk))
    sink.put(1, dot_tn(x_rows, dv))


def feed_grads_kernel(info_ref, h2_ref, gu_ref, f_ref, e3_ref, *refs, plain):
    sink_refs, (dw_ref,) = (refs[:1], refs[1:]) if plain else (refs[:2], refs[2:])
    info = RowInfo(info_ref)
    sink = PlainSink(*sink_refs) if plain else PieceSink(*sink_refs, dw_ref, info.me, info.side)
    width = h2_ref.shape[1]
    parts = gu_ref.shape[1] // width
    for k in range(parts):
        sink.put(k, dot_tn(h2_ref[...], gu_ref[:, k * width : (k + 1) * width]))
    sink.put(parts, dot_tn(f_ref[...], e3_ref[...]))


def map_grads_kernel(
    info_ref, a_ref, e1_ref, ac_ref, e2_ref, h1_ref, dqc_ref, dwc_ref, x_ref, dq_ref, sums_ref,
    csum_ref, *refs, plain,
):
    sink_refs, (dw_ref,) = (refs[:1], refs[1:]) if plain else (refs[:2], refs[2:])
    info = RowInfo(info_ref)
    sink = PlainSink(*sink_refs) if plain else PieceSink(*sink_refs, dw_ref, info.me, info.side)
    width = a_ref.shape[1]
    sink.put(0, dot_tn(a_ref[...], e1_ref[...]))
    sink.put(1, dot_tn(ac_ref[...], e2_ref[...]))
    sink.put(2, dot_tn(h1_ref[...], dqc_ref[...]))
    sink.put(3, dwc_ref[:, :width])
    sink.put(4, dwc_ref[:, width:])
    sink.put(5, dot_tn(x_ref[...], dq_ref[...]))
    put_small(sink, 6, dw_ref, sums_ref[...], csum_ref, dq_ref[...])


def put_small(sink, block, dw_ref, sums, csum_ref, dq):
    dw_ref[...] = jnp.zeros(dw_ref.shape, f32)
    row = lax.broadcasted_iota(jnp.int32, sums.shape, 0)
    sums = jnp.where(row == 3, column_sum(dq), sums)
    lanes = csum_ref.shape[1] // 8
    for yh in range(2):
        base = yh * half_rows
        dw_ref[base : base + 16, 0:lanes] = sums[:, yh * lanes : (yh + 1) * lanes]
        for k in range(4):
            start = yh * 4 * lanes + k * lanes
            dw_ref[base + 16 + k : base + 17 + k, 0:lanes] = csum_ref[:, start : start + lanes]
    if isinstance(sink, PlainSink):
        sink.plain[block] = dw_ref[...].astype(bf16)
    else:
        sink.emit(block, half_rows, 0)


def place_kernel(info_ref, *refs, places):
    sources, outs = refs[:4], refs[4:]
    info = RowInfo(info_ref)
    planes = sources[0].shape[0]
    piece = half_rows // (4 * planes)
    for s in range(planes):
        for bits in range(4):
            owner = info.me ^ (4 * s + bits)
            source = sources[(bits >> 1) + 2 * (bits & 1)]
            for block, (number, kind, k) in enumerate(places):
                rows = source[s, block * piece : (block + 1) * piece, :].astype(f32)
                width = rows.shape[1]
                base = k * half_rows if kind == "rows" else 0
                at = pl.ds(pl.multiple_of(base + owner * piece, piece), piece)
                if kind == "lead":
                    outs[number][k, at, :] = rows
                elif kind == "cols":
                    outs[number][at, k * width : (k + 1) * width] = rows
                else:
                    outs[number][at, :] = rows


def place_maps_kernel(
    info_ref, own_ref, other_ref, own_core_ref, other_core_ref, ins_ref, outs_ref, gain_ref, bias_ref,
    shift_ref, rest_ref,
):
    place_kernel(
        info_ref, own_ref, other_ref, own_core_ref, other_core_ref, ins_ref, outs_ref, rest_ref,
        places=[(1, "lead", 0), (1, "lead", 1)]
        + [(0, "lead", k) for k in (3, 4, 5, 0)]
        + [(2, "rows", 0), (0, "lead", 1), (0, "lead", 2)],
    )
    lanes = gain_ref.shape[1]
    gain_ref[...] = rest_ref[0:3, 0:lanes]
    bias_ref[...] = rest_ref[3:13, 0:lanes]
    shift_ref[...] = rest_ref[16:20, 0:lanes]


def call_kernel(kernel, inputs, outputs, scratch, name, micros, in_place=()):
    vmem = pl.BlockSpec(memory_space=pltpu.VMEM)
    smem = pl.BlockSpec(memory_space=pltpu.SMEM)
    return pl.pallas_call(
        kernel,
        in_specs=[smem]
        + [
            pl.BlockSpec(memory_space=pl.ANY) if index in in_place else vmem
            for index in range(1, len(inputs))
        ],
        out_specs=[vmem] * len(outputs),
        out_shape=[jax.ShapeDtypeStruct(*entry) for entry in outputs],
        scratch_shapes=[pltpu.VMEM(*entry) if isinstance(entry, tuple) else entry for entry in scratch],
        compiler_params=pltpu.CompilerParams(vmem_limit_bytes=vmem_bytes),
        cost_estimate=pl.CostEstimate(
            flops=int(micros * 1e9), transcendentals=0, bytes_accessed=int(micros * 1e4)
        ),
        name=name,
    )(*inputs)


def exchange(value, bits):
    count = lax.axis_size("ctx")
    return lax.ppermute(value, "ctx", [(i, i ^ bits) for i in range(count)])


def swap_side(value):
    return lax.ppermute(value, "fsdp", [(0, 1), (1, 0)])


def after(value, *others):
    return lax.optimization_barrier((value,) + others)[0]


def fetch_planes(value):
    planes = lax.axis_size("ctx") // 4
    return [value] + [exchange(value, 4 * s) for s in range(1, planes)]


def fetch_chips(chunks):
    return [chunks, exchange(chunks, 2)]


def fetch_cores(pair):
    return pair + [exchange(chunks, 1) for chunks in pair]


def core_part(shard, axis):
    rows = shard.shape[axis] // 2
    return lax.dynamic_slice_in_dim(shard, (lax.axis_index("ctx") % 2) * rows, rows, axis)


def add_cores(keep, send):
    other = exchange(send, 1)
    return keep[0].astype(f32) + other[0].astype(f32), (
        keep[1].astype(f32) + other[1].astype(f32)
    ).astype(bf16)


def add_sides(kept, sent):
    return kept + swap_side(sent).astype(f32)


def add_chips(part, low):
    return part[0] + exchange(low, 2).astype(f32)


def low_planes(part):
    return [part[s].astype(bf16) for s in range(1, part.shape[0])]


def add_planes(part, low):
    total = part[0]
    for s, sent in enumerate(low):
        total = total + exchange(sent, 4 * (s + 1)).astype(f32)
    return total


def spread_planes(low):
    planes = lax.axis_size("ctx") // 4
    return [low] + [exchange(low, 4 * s) for s in range(1, planes)]


def spread_chips(chunks, before=None):
    own = jnp.stack(chunks)
    other = exchange(own, 2)
    sent = [own, other] if before is None else [after(own, before), after(other, before)]
    return [own, other] + [exchange(chunk, 1) for chunk in sent]


def zigzag_perms(count):
    def worker(block):
        return block if block < count else 2 * count - 1 - block

    first = [(owner, worker(2 * owner)) for owner in range(count)]
    second = [(owner, worker(2 * owner + 1)) for owner in range(count)]
    return first, second


def body(
    tokens, memory, token_seg, memory_seg, out_grad,
    in_proj, out_proj, ffn_in, ffn_out, norm_gain, bias_rows, ffn_bias,
):
    count = lax.axis_size("ctx")
    sides = lax.axis_size("fsdp")
    planes = count // 4
    plain = sides != 2
    me = lax.axis_index("ctx")
    side = lax.axis_index("fsdp")
    row_count, width = tokens.shape[1], tokens.shape[2]
    mem_count = memory.shape[1]
    half = row_count // 2
    scale = 1.0 / math.sqrt(width // HEADS)
    factor = scale * math.log2(math.e)
    total = row_count * count
    mem_total = mem_count * count
    near, far = planes // 2, planes - planes // 2

    x_planes = fetch_planes(tokens[0])
    small = jnp.concatenate(
        [norm_gain, bias_rows, ffn_bias.reshape(-1, norm_gain.shape[1])], axis=0
    ).astype(bf16)
    maps_low = jnp.concatenate([in_proj, out_proj], axis=0).astype(bf16)
    up_low, down_low = ffn_in.astype(bf16), ffn_out.astype(bf16)
    if plain:
        small = lax.all_gather(small, "fsdp").astype(f32)
        whole = lax.all_gather(maps_low, "fsdp", axis=1, tiled=True)
        self_maps = (whole,)
        late_maps = (
            whole, lax.all_gather(up_low, "fsdp", axis=0, tiled=True),
            lax.all_gather(down_low, "fsdp", axis=0, tiled=True),
        )
    else:
        small_rows = small.shape[0]
        pad = jnp.zeros((32 - small_rows, small.shape[1]), bf16)
        sent = jnp.concatenate(
            [
                core_part(in_proj[0:3], 1).astype(bf16).reshape(-1, width),
                jnp.concatenate([small, pad], axis=0).reshape(-1, width),
            ],
            axis=0,
        )
        fetched = swap_side(sent)
    x_near = fetch_chips(jnp.stack(x_planes[:near]))
    if not plain:
        ready = after(fetched, x_near[1])
        table_rows = ready[-pad.shape[1] * 32 // width :].reshape(32, -1)[:small_rows]
        small = jnp.stack([small, table_rows])
        small = jnp.where(side == 0, small, small[::-1]).astype(f32)
        self_maps = (maps_low, ready, exchange(ready, 1))
        up_part = core_part(after(ffn_in, sent), 0).astype(bf16)
        late_parts = [
            core_part(in_proj[3:6], 1).astype(bf16).reshape(-1, width),
            core_part(after(out_proj, sent), 1).astype(bf16).reshape(-1, width),
            core_part(after(ffn_out, sent), 0).astype(bf16),
        ]
        late_parts += [
            up_part[:, k * width : (k + 1) * width] for k in range(up_part.shape[1] // width)
        ]
        late_sent = jnp.concatenate(late_parts, axis=0)
        late = swap_side(after(late_sent, fetched))
    started = x_near[0] if plain else fetched
    x_far = fetch_chips(jnp.stack([after(chunk, started) for chunk in x_planes[near:]]))

    perm_first, perm_second = zigzag_perms(count)
    even = me % 2 == 0
    first_sent = small if plain else sent
    rows_in = jnp.stack([after(tokens[0], first_sent, x_near[0]), out_grad[0]])
    one = lax.ppermute(rows_in[:, :half], "ctx", perm_first)
    two = lax.ppermute(rows_in[:, half:], "ctx", perm_second)
    rows_in = jnp.where(
        even, jnp.concatenate([one, two], axis=1), jnp.concatenate([two, one], axis=1)
    )
    x_rows, g_rows = rows_in[0], rows_in[1]

    table = small[:, 0:13].transpose(1, 0, 2).reshape(13, width)
    gains, biases = table[0:3], table[3:13]
    ffn_shift = small[:, 13:].reshape(1, -1)

    m_all = lax.all_gather(memory[0], "ctx", axis=0, tiled=True)

    segs, mem_segs = after(token_seg[0], first_sent), after(memory_seg[0], first_sent)
    step = jnp.arange(half, dtype=jnp.int32)
    row_pos = jnp.concatenate([me * half + step, (2 * count - 1 - me) * half + step])
    row_seg = jnp.concatenate(
        [
            lax.dynamic_slice_in_dim(segs, me * half, half),
            lax.dynamic_slice_in_dim(segs, (2 * count - 1 - me) * half, half),
        ]
    )

    def below(keys, closed):
        hits = keys[None, :] <= row_seg[:, None] if closed else keys[None, :] < row_seg[:, None]
        return jnp.sum(hits, axis=1, dtype=jnp.int32)

    ones = jnp.ones_like(row_pos)
    info = jnp.stack(
        [
            below(segs, False), row_pos, below(mem_segs, False), below(mem_segs, True) - 1,
            below(segs, True) - 1, me * ones, side * ones, ones,
        ]
    )
    cols = info.T

    tile = width // PAIRS
    column = ((PAIRS, row_count, 1), f32)
    square = ((PAIRS, row_count, tile), f32)
    two_squares = ((2, PAIRS, row_count, tile), f32)
    rows_low = ((row_count, width), bf16)
    rows_full = ((row_count, width), f32)
    kv_rows_shape = ((row_count, 2 * width), bf16)

    x_near = fetch_cores(x_near)
    x_near[0] = after(x_near[0], x_far[0], up_low, down_low)
    wide = ((PAIRS, row_count, 2 * tile), f32)
    q_rows, kv_rows, kv_near, w_self, top, weights = call_kernel(
        lambda *refs: first_forward_kernel(
            *refs, factor=factor, planes=near, shards=len(self_maps)
        ),
        (info, x_rows, biases, cols, *self_maps, *x_near),
        (
            rows_low, kv_rows_shape, ((4 * near * row_count, 2 * width), bf16),
            ((3, width, width), bf16), rows_full, rows_full,
        ),
        [wide],
        "first_forward",
        10,
    )
    x_far = fetch_cores([after(chunks, top) for chunks in x_far])
    a_rows, log_rows, kv_far = call_kernel(
        lambda *refs: second_forward_kernel(*refs, factor=factor, planes=far),
        (info, kv_near, q_rows, biases, cols, w_self, top, weights, *x_far),
        (rows_full, ((HEADS, row_count), f32), ((4 * far * row_count, 2 * width), bf16)),
        [
            wide, column, column, square, rows_full, ((4 * near * row_count, 2 * width), bf16),
            pltpu.SemaphoreType.DMA,
        ],
        "second_forward",
        10,
        (1,),
    )
    if not plain:
        late = after(late, a_rows)
        late_maps = (maps_low, up_low, down_low, late, exchange(late, 1))
    ff_width = ffn_in.shape[1]
    ff_rows = ((row_count, ff_width), bf16)
    by_head = ((HEADS, row_count), f32)
    kvc_shape = ((mem_total, 2 * width), bf16)
    sums_shape = ((16, width), f32)
    whole_maps = [] if plain else [((width, ff_width), bf16), ((ff_width, width), bf16)]
    (
        out_rows, a_low, h1_low, h2_low, act, e3, gu, e2, ac_low, gr2, r1, qc, cross, cross_log,
        kvc, sums, csum, w_cross,
    ) = call_kernel(
        lambda *refs: middle_forward_kernel(
            *refs, factor=factor, shards=len(self_maps), cross_rows=2 * mem_count
        ),
        (info, x_rows, a_rows, g_rows, cols, gains, biases, ffn_shift, m_all, *late_maps),
        (
            rows_full, rows_low, rows_low, rows_low, ff_rows, rows_low, ff_rows, rows_low, rows_low,
            rows_full, rows_full, rows_low, rows_full, by_head, kvc_shape, sums_shape,
            ((1, ff_width), f32), ((5, width, width), bf16),
        ),
        [wide, column, column, square, rows_full, *whole_maps],
        "middle_forward",
        25,
    )

    def sink_shapes(blocks):
        if plain:
            return [((blocks, width, width), bf16)]
        return [((2, 2, planes, blocks * (half_rows // count), width), bf16)] * 2

    feed = call_kernel(
        lambda *refs: feed_grads_kernel(*refs, plain=plain),
        (info, h2_low, gu, act, e3),
        sink_shapes(8),
        [((ff_width, width), f32)],
        "feed_grads",
        5,
    )
    gr2 = after(gr2, *feed)
    e1, dqc, ga, gr1, delta, dkvc, sums = call_kernel(
        lambda *refs: middle_backward_kernel(
            *refs, factor=factor, scale=scale, cross_rows=2 * mem_count
        ),
        (
            info, a_rows, log_rows, info, gains, w_cross, e2, gr2, r1, qc, cross, cross_log, kvc,
            sums,
        ),
        (
            rows_low, rows_low, ((row_count + chunk_rows, width), bf16), rows_full, by_head,
            kvc_shape, sums_shape,
        ),
        [((PAIRS, tile, row_count), f32)],
        "middle_backward",
        14,
    )
    g_planes = fetch_planes(ga)
    if not plain:
        feed = add_cores(*feed)
        dkvc = after(dkvc, feed[1])
    mem_part, dwc = call_kernel(
        lambda *refs: memory_grads_kernel(*refs, cross_block=2 * mem_count),
        (info, m_all, w_cross, dkvc),
        (((mem_total, width), bf16), ((width, 2 * width), bf16)),
        [((width, 2 * width), f32)],
        "memory_grads",
        5,
    )
    g_near = fetch_chips(jnp.stack([after(chunk, mem_part) for chunk in g_planes[:near]]))
    (dq,) = call_kernel(
        lambda *refs: query_backward_kernel(*refs, factor=factor, scale=scale, planes=near),
        (info, after(q_rows, g_near[0]), ga, kv_near, kv_far, log_rows, delta, cols),
        (rows_low,),
        [square, square, square],
        "query_backward",
        20,
    )
    g_far = fetch_chips(jnp.stack([after(chunk, dq) for chunk in g_planes[near:]]))
    g_near = fetch_cores([after(chunks, dq) for chunks in g_near])
    maps = call_kernel(
        lambda *refs: map_grads_kernel(*refs, plain=plain),
        (info, a_low, e1, ac_low, e2, after(h1_low, g_far[0], g_near[1]), dqc, dwc, x_rows, dq, sums, csum),
        sink_shapes(7),
        [((width, width), f32)],
        "map_grads",
        6,
    )
    (q_all,) = call_kernel(
        lambda *refs: project_kernel(*refs, planes=near),
        (info, after(w_self, maps[0]), biases, *x_near, *x_far),
        (((total, width), bf16),),
        [],
        "project",
        7,
    )
    if not plain:
        maps = add_cores(*maps)
        feed = add_sides(*feed)
        feed_low = feed[1].astype(bf16)
        kv_rows = after(kv_rows, maps[1], feed_low)
    mem_part = after(mem_part, g_far[1])
    memory_grad = lax.psum_scatter(mem_part, "ctx", scatter_dimension=0, tiled=True).astype(f32)
    g_far = fetch_cores([after(chunks, q_all) for chunks in g_far])
    dk_part, dv_part = call_kernel(
        lambda *refs: key_backward_kernel(
            *refs, factor=factor, scale=scale, planes=near, part=0, last=False,
            total_planes=planes,
        ),
        (info, kv_rows, q_all, cols, *g_near),
        [two_squares, two_squares],
        [
            ((4 * near * row_count, width), bf16), ((8 * near, 2 * HEADS, half), f32),
        ],
        "key_backward",
        8,
    )
    if not plain:
        feed = add_chips(feed, feed_low)
        feed_low = low_planes(feed)
        dk_part = after(dk_part, *feed_low)
    dk, dv = call_kernel(
        lambda *refs: key_backward_kernel(
            *refs, factor=factor, scale=scale, planes=far, part=1, last=True, total_planes=planes
        ),
        (info, kv_rows, q_all, cols, dk_part, dv_part, *g_far),
        [rows_low, rows_low],
        [
            ((4 * far * row_count, width), bf16), ((8 * far, 2 * HEADS, half), f32),
            two_squares, two_squares,
        ],
        "key_backward_last",
        12,
    )
    if not plain:
        feed = add_planes(feed, feed_low).astype(bf16)
        maps = add_sides(*maps)
        maps_low = maps[1].astype(bf16)
        dk = after(dk, feed, maps_low)
    tok_rows, *last = call_kernel(
        lambda *refs: self_grads_kernel(*refs, plain=plain),
        (info, x_rows, gr1, dq, dk, dv, w_self),
        [rows_low] + sink_shapes(2),
        [((width, width), f32)],
        "self_grads",
        4,
    )

    back_first = [(to, owner) for owner, to in perm_first]
    back_second = [(to, owner) for owner, to in perm_second]

    rows_out = jnp.stack([out_rows.astype(bf16), tok_rows])
    half_one = jnp.where(even, rows_out[:, :half], rows_out[:, half:])
    half_two = jnp.where(even, rows_out[:, half:], rows_out[:, :half])
    rows_out = jnp.concatenate(
        [lax.ppermute(half_one, "ctx", back_first), lax.ppermute(half_two, "ctx", back_second)],
        axis=1,
    ).astype(f32)
    layer_out, tokens_grad = rows_out[0], rows_out[1]
    lanes = width // 2
    if plain:

        def owned(matrix, axis):
            part = lax.psum_scatter(matrix, "fsdp", scatter_dimension=axis, tiled=True)
            return lax.psum(part, "ctx").astype(f32)

        feed, maps, last = feed[0], maps[0], last[0]
        ins = owned(jnp.concatenate([maps[5:6], last, maps[2:5]], axis=0), 1)
        outs = owned(maps[0:2], 1)
        up = owned(jnp.concatenate([feed[k] for k in range(4)], axis=1), 0)
        down = owned(feed[4:8].reshape(-1, width), 0)
        rest = jnp.stack([maps[6, 0:half_rows, 0:lanes], maps[6, half_rows:, 0:lanes]], axis=1)
        table = owned(rest[0:13].reshape(13, width).astype(f32), 1)
        shift = owned(rest[16:20].transpose(1, 0, 2).reshape(-1).astype(f32), 0)
        gain_sums, bias_sums = table[0:3], table[3:13]
    else:
        feed_planes = spread_planes(feed)
        last = add_sides(*add_cores(*last))
        last_low = after(last[1].astype(bf16), *feed_planes[1:])
        feed_own = jnp.stack(feed_planes)
        feed_other = exchange(feed_own, 2)
        last = add_chips(last, last_low)
        maps = add_chips(maps, maps_low)
        maps = add_planes(maps, low_planes(maps)).astype(bf16)
        last = add_planes(last, [after(low, maps) for low in low_planes(last)]).astype(bf16)
        up, down = call_kernel(
            lambda *refs: place_kernel(
                *refs,
                places=[(0, "cols", k) for k in range(4)] + [(1, "rows", k) for k in range(4)],
            ),
            (info, feed_own, feed_other, exchange(feed_own, 1), exchange(feed_other, 1)),
            ((ffn_in.shape, f32), (ffn_out.shape, f32)),
            [],
            "place_feed",
            4,
        )
        maps = jnp.concatenate([maps, after(last, feed_other)], axis=0)
        ins, outs, gain_sums, bias_sums, shift = call_kernel(
            place_maps_kernel,
            (info, *spread_chips(spread_planes(maps), up)),
            (
                (in_proj.shape, f32), (out_proj.shape, f32), ((3, lanes), f32), ((10, lanes), f32),
                ((4, lanes), f32),
            ),
            [((half_rows, width), f32)],
            "place_maps",
            4,
        )
        shift = shift.reshape(-1)
    return (
        layer_out[None], tokens_grad[None], memory_grad[None], ins, outs, up, down,
        gain_sums, bias_sums, shift,
    )


def solution(mesh):
    rows = P("fsdp", "ctx", None)
    params = (
        P(None, "fsdp", None), P(None, "fsdp", None), P("fsdp", None), P("fsdp", None),
        P(None, "fsdp"), P(None, "fsdp"), P("fsdp"),
    )
    return jax.shard_map(
        body,
        mesh=mesh,
        in_specs=(rows, rows, P("fsdp", None), P("fsdp", None), rows) + params,
        out_specs=(rows, rows, rows) + params,
        check_vma=False,
    )
```

profile of v0, /device:TPU:9, one launch (start us, length us, event | category | flops | bytes accessed | tf_op | source)
XLA Modules:
  0.0 363.8 jit_solution(1106776894854873923)
XLA Ops:
  13.0 3.0 fusion.37
  38.9 4.7 %collective-permute-start.1 = (bf16[2,128,512]{2,1,0:T(8,128)(2,1)}, bf16[2,128,512]{2,1,0:T(8,128)(2,1)S(1)}, u32[]{:S(2)}, u32[]{:S(2)}) collective-permute-start(bf16[2,128,512]{2,1,0:T(8,128)(2,1)} %get-tuple-element.215), channel_id=1, source_target_pairs={{0,0},{2,4},{4,8},{6,12},{8,16},{10,20},{12,24},{14,28},{16,30},{1... | collective-permute-start | bytes 786440 | tf_op jit(solution)/shard_map/ppermute | solution.py:1078
  55.7 6.4 %collective-permute-done.2 = bf16[2,128,512]{2,1,0:T(8,128)(2,1)} collective-permute-done((bf16[2,128,512]{2,1,0:T(8,128)(2,1)S(1)}, bf16[2,128,512]{2,1,0:T(8,128)(2,1)}, u32[]{:S(2)}, u32[]{:S(2)}) %collective-permute-start.2) | collective-permute-done | bytes 262176 | tf_op jit(solution)/shard_map/ppermute | solution.py:1079
  68.6 13.7 %first_forward.1 = (bf16[256,512]{1,0:T(8,128)(2,1)}, bf16[256,1024]{1,0:T(8,128)(2,1)}, bf16[2048,1024]{1,0:T(8,128)(2,1)}, bf16[3,512,512]{2,1,0:T(8,128)(2,1)...) custom-call(s32[8,256]{1,0:T(8,128)} %copy-done.18, bf16[256,512]{1,0:T(8,128)(2,1)} %get-tuple-element.214.refs_1_.refs_8_, ...), custom_call_target="tpu_custom_call" | custom-call | flops 10000000000 | bytes 100000 | tf_op jit(solution)/shard_map/first_forward/pallas_call | solution.py:913
  85.8 10.9 %second_forward.1 = (f32[256,512]{1,0:T(8,128)}, f32[8,256]{1,0:T(8,128)}, bf16[2048,1024]{1,0:T(8,128)(2,1)}) custom-call(s32[8,256]{1,0:T(8,128)} %copy-done.18, bf16[2048,1024]{1,0:T(8,128)(2,1)} %get-tuple-element.109.refs_1_.refs_3_, bf16[256,512]{1,0:T(8,128)(2,1)} %get-tuple-element.147.refs_2_.refs_1_, f32[10,512]{1,0:T(8,128)} %bitcast.154, ...), custom_call_target="tpu_custom_call" | custom-call | flops 10000000000 | bytes 100000 | tf_op jit(solution)/shard_map/second_forward/pallas_call | solution.py:913
  101.8 16.2 %middle_forward.1 = (f32[256,512]{1,0:T(8,128)}, bf16[256,512]{1,0:T(8,128)(2,1)}, bf16[256,512]{1,0:T(8,128)(2,1)}, bf16[256,512]{1,0:T(8,128)(2,1)}, bf16[256,...) custom-call(s32[8,256]{1,0:T(8,128)} %copy-done.18, ...), custom_call_target="tpu_custom_call" | custom-call | flops 24999999488 | bytes 250000 | tf_op jit(solution)/shard_map/middle_forward/pallas_call | solution.py:913
  118.0 5.3 %feed_grads.1 = (bf16[2,2,4,128,512]{4,3,2,1,0:T(8,128)(2,1)}, bf16[2,2,4,128,512]{4,3,2,1,0:T(8,128)(2,1)}) custom-call(s32[8,256]{1,0:T(8,128)} %copy-done.18, bf16[256,512]{1,0:T(8,128)(2,1)} %get-tuple-element.127.refs_1_, bf16[256,2048]{1,0:T(8,128)(2,1)} %get-tuple-element.128.refs_2_, bf16[256,2048]{1,0:T(8,128)(2,1)} %get-tuple-element.129.refs_3_, ...), custom_call_target="tpu_custom_call" | custom-call | flops 5000000000 | bytes 50000 | tf_op jit(solution)/shard_map/feed_grads/pallas_call | solution.py:913
  123.7 15.0 %middle_backward.1 = (bf16[256,512]{1,0:T(8,128)(2,1)}, bf16[256,512]{1,0:T(8,128)(2,1)}, bf16[288,512]{1,0:T(8,128)(2,1)}, f32[256,512]{1,0:T(8,128)}, f32[8,25...) custom-call(s32[8,256]{1,0:T(8,128)} %copy-done.18, f32[256,512]{1,0:T(8,128)} %get-tuple-element.116.refs_2_.refs_1_, ...), custom_call_target="tpu_custom_call" | custom-call | flops 14000000000 | bytes 140000 | tf_op jit(solution)/shard_map/middle_backward/pallas_call | solution.py:913
  138.7 4.8 %collective-permute-start.18 = (bf16[288,512]{1,0:T(8,128)(2,1)}, bf16[288,512]{1,0:T(8,128)(2,1)S(1)}, u32[]{:S(2)}, u32[]{:S(2)}) collective-permute-start(bf16[288,512]{1,0:T(8,128)(2,1)} %get-tuple-element.145.refs_2_), channel_id=1, source_target_pairs={{0,24},{2,26},{4,28},{6,30},{8,16},{10,18},{12,20},{14,22},{16,8},... | collective-permute-start | bytes 884744 | tf_op jit(solution)/shard_map/ppermute | solution.py:933
  143.5 9.1 %collective-permute-start.17 = (bf16[288,512]{1,0:T(8,128)(2,1)}, bf16[288,512]{1,0:T(8,128)(2,1)S(1)}, u32[]{:S(2)}, u32[]{:S(2)}) collective-permute-start(bf16[288,512]{1,0:T(8,128)(2,1)} %get-tuple-element.145.refs_2_), channel_id=1, source_target_pairs={{0,16},{2,18},{4,20},{6,22},{8,24},{10,26},{12,28},{14,30},{16,0},... | collective-permute-start | bytes 884744 | tf_op jit(solution)/shard_map/ppermute | solution.py:933
  154.2 8.0 %memory_grads.1 = (bf16[2048,512]{1,0:T(8,128)(2,1)}, bf16[512,1024]{1,0:T(8,128)(2,1)}) custom-call(s32[8,256]{1,0:T(8,128)} %copy-done.18, bf16[2048,512]{1,0:T(8,128)(2,1)} %bitcast.169, bf16[5,512,512]{2,1,0:T(8,128)(2,1)} %get-tuple-element.124.refs_5_.refs_2_, bf16[2048,1024]{1,0:T(8,128)(2,1)} %get-tuple-element.143.refs_3_), custom_call_target="tpu_custom_call" | custom-call | flops 5000000000 | bytes 50000 | tf_op jit(solution)/shard_map/memory_grads/pallas_call | solution.py:913
  162.2 3.7 %collective-permute-done.16 = bf16[288,512]{1,0:T(8,128)(2,1)S(1)} collective-permute-done((bf16[288,512]{1,0:T(8,128)(2,1)}, bf16[288,512]{1,0:T(8,128)(2,1)S(1)}, u32[]{:S(2)}, u32[]{:S(2)}) %collective-permute-start.16) | collective-permute-done | bytes 294944 | tf_op jit(solution)/shard_map/ppermute | solution.py:933
  166.8 18.0 %query_backward.1.refs_9_.refs_3_ = bf16[256,512]{1,0:T(8,128)(2,1)} custom-call(s32[8,256]{1,0:T(8,128)} %copy-done.18, bf16[256,512]{1,0:T(8,128)(2,1)} %get-tuple-element.147.refs_2_.refs_1_, bf16[288,512]{1,0:T(8,128)(2,1)} %get-tuple-element.145.refs_2_, bf16[2048,1024]{1,0:T(8,128)(2,1)} %get-tuple-element.109.refs_1_.refs_3_, ...), custom_call_target="tpu_custom_call" | custom-call | flops 20000000000 | bytes 200000 | tf_op jit(solution)/shard_map/query_backward/pallas_call | solution.py:913
  185.8 6.2 %collective-permute-done.21 = bf16[2,4,128,512]{3,2,1,0:T(8,128)(2,1)} collective-permute-done((bf16[2,4,128,512]{3,2,1,0:T(8,128)(2,1)S(1)}, bf16[2,4,128,512]{3,2,1,0:T(8,128)(2,1)}, u32[]{:S(2)}, u32[]{:S(2)}) %collective-permute-start.21) | collective-permute-done | bytes 1048608 | tf_op jit(solution)/shard_map/ppermute | solution.py:937
  195.7 5.1 %map_grads.1 = (bf16[2,2,4,112,512]{4,3,2,1,0:T(8,128)(2,1)}, bf16[2,2,4,112,512]{4,3,2,1,0:T(8,128)(2,1)}) custom-call(s32[8,256]{1,0:T(8,128)} %copy-done.18, bf16[256,512]{1,0:T(8,128)(2,1)} %get-tuple-element.151.refs_1_, bf16[256,512]{1,0:T(8,128)(2,1)} %get-tuple-element.152.refs_2_, bf16[256,512]{1,0:T(8,128)(2,1)} %get-tuple-element.153.refs_3_, ...), custom_call_target="tpu_custom_call" | custom-call | flops 6000000000 | bytes 60000 | tf_op jit(solution)/shard_map/map_grads/pallas_call | solution.py:913
  202.5 5.8 %collective-permute-done.24 = bf16[4,128,512]{2,1,0:T(8,128)(2,1)} collective-permute-done((bf16[4,128,512]{2,1,0:T(8,128)(2,1)}, bf16[4,128,512]{2,1,0:T(8,128)(2,1)}, u32[]{:S(2)}, u32[]{:S(2)}) %collective-permute-start.24) | collective-permute-done | bytes 524320 | tf_op jit(solution)/shard_map/ppermute | solution.py:933
  210.6 2.8 collective-permute-start.30
  215.7 5.2 %collective-permute-done.25.refs_7_ = bf16[2,288,512]{2,1,0:T(8,128)(2,1)S(1)} collective-permute-done((bf16[2,288,512]{2,1,0:T(8,128)(2,1)}, bf16[2,288,512]{2,1,0:T(8,128)(2,1)S(1)}, u32[]{:S(2)}, u32[]{:S(2)}) %collective-permute-start.25) | collective-permute-done | bytes 589856 | tf_op jit(solution)/shard_map/ppermute | solution.py:933
  224.8 7.0 %project.1.refs_2_ = bf16[4096,512]{1,0:T(8,128)(2,1)} custom-call(s32[8,256]{1,0:T(8,128)} %copy-done.18, bf16[3,512,512]{2,1,0:T(8,128)(2,1)} %get-tuple-element.166.refs_5_.refs_1_.refs_6_, f32[10,512]{1,0:T(8,128)} %bitcast.156, bf16[2,256,512]{2,1,0:T(8,128)(2,1)} %copy-done.11, bf16[2,256,512]{2,1,0:T(8,128)(2,1)} %collective-permute-done.4.refs_8_.refs_4_, ...), custom_call_target="tpu_custom_call" | custom-call | flops 7000000000 | bytes 70000 | tf_op jit(solution)/shard_map/project/pallas_call | solution.py:913
  236.3 13.3 %key_backward.1 = (f32[2,4,256,128]{3,2,1,0:T(8,128)}, f32[2,4,256,128]{3,2,1,0:T(8,128)}) custom-call(s32[8,256]{1,0:T(8,128)} %copy-done.18, bf16[256,1024]{1,0:T(8,128)(2,1)} %get-tuple-element.165.refs_1_, bf16[4096,512]{1,0:T(8,128)(2,1)} %project.1.refs_2_, s32[256,8]{1,0:T(8,128)} %copy.30.refs_3_.refs_4_.refs_7_, ...), custom_call_target="tpu_custom_call" | custom-call | flops 8000000000 | bytes 80000 | tf_op jit(solution)/shard_map/key_backward/pallas_call | solution.py:913
  249.6 11.6 %key_backward_last.1 = (bf16[256,512]{1,0:T(8,128)(2,1)}, bf16[256,512]{1,0:T(8,128)(2,1)}) custom-call(s32[8,256]{1,0:T(8,128)} %copy-done.18, bf16[256,1024]{1,0:T(8,128)(2,1)} %get-tuple-element.165.refs_1_, bf16[4096,512]{1,0:T(8,128)(2,1)} %project.1.refs_2_, s32[256,8]{1,0:T(8,128)} %copy.30.refs_3_.refs_4_.refs_7_, ...), custom_call_target="tpu_custom_call" | custom-call | flops 12000000000 | bytes 120000 | tf_op jit(solution)/shard_map/key_backward_last/pallas_call | solution.py:913
  263.4 3.8 %self_grads.1 = (bf16[256,512]{1,0:T(8,128)(2,1)}, bf16[2,2,4,32,512]{4,3,2,1,0:T(8,128)(2,1)}, bf16[2,2,4,32,512]{4,3,2,1,0:T(8,128)(2,1)}) custom-call(s32[8,256]{1,0:T(8,128)} %copy-done.18, bf16[256,512]{1,0:T(8,128)(2,1)} %get-tuple-element.214.refs_1_.refs_8_, f32[256,512]{1,0:T(8,128)} %get-tuple-element.140.refs_2_, ...), custom_call_target="tpu_custom_call" | custom-call | flops 4000000000 | bytes 40000 | tf_op jit(solution)/shard_map/self_grads/pallas_call | solution.py:913
  271.6 7.3 %collective-permute-done.42 = bf16[128,512]{1,0:T(8,128)(2,1)} collective-permute-done((bf16[128,512]{1,0:T(8,128)(2,1)S(1)}, bf16[128,512]{1,0:T(8,128)(2,1)}, u32[]{:S(2)}, u32[]{:S(2)}) %collective-permute-start.42) | collective-permute-done | bytes 131104 | tf_op jit(solution)/shard_map/ppermute | solution.py:933
  283.9 3.4 collective-permute-start.35
  290.6 5.5 %collective-permute-done.37 = bf16[112,512]{1,0:T(8,128)(2,1)S(1)} collective-permute-done((bf16[112,512]{1,0:T(8,128)(2,1)S(1)}, bf16[112,512]{1,0:T(8,128)(2,1)S(1)}, u32[]{:S(2)}, u32[]{:S(2)}) %collective-permute-start.37) | collective-permute-done | bytes 114720 | tf_op jit(solution)/shard_map/ppermute | solution.py:933
  296.7 3.2 collective-permute-start.45
  302.6 4.4 %collective-permute-done.46 = bf16[32,512]{1,0:T(8,128)(2,1)S(1)} collective-permute-done((bf16[32,512]{1,0:T(8,128)(2,1)S(1)}, bf16[32,512]{1,0:T(8,128)(2,1)S(1)}, u32[]{:S(2)}, u32[]{:S(2)}) %collective-permute-start.46) | collective-permute-done | bytes 32800 | tf_op jit(solution)/shard_map/ppermute | solution.py:933
  312.1 5.1 %collective-permute-done.49 = bf16[144,512]{1,0:T(8,128)(2,1)S(1)} collective-permute-done((bf16[144,512]{1,0:T(8,128)(2,1)S(1)}, bf16[144,512]{1,0:T(8,128)(2,1)S(1)}, u32[]{:S(2)}, u32[]{:S(2)}) %collective-permute-start.49) | collective-permute-done | bytes 147488 | tf_op jit(solution)/shard_map/ppermute | solution.py:933
  318.8 6.8 %collective-permute-done.50 = bf16[144,512]{1,0:T(8,128)(2,1)S(1)} collective-permute-done((bf16[144,512]{1,0:T(8,128)(2,1)S(1)}, bf16[144,512]{1,0:T(8,128)(2,1)S(1)}, u32[]{:S(2)}, u32[]{:S(2)}) %collective-permute-start.50) | collective-permute-done | bytes 147488 | tf_op jit(solution)/shard_map/ppermute | solution.py:933
  332.8 3.9 %place_feed.1 = (f32[256,2048]{1,0:T(8,128)}, f32[1024,512]{1,0:T(8,128)}) custom-call(s32[8,256]{1,0:T(8,128)} %copy-done.18, bf16[4,128,512]{2,1,0:T(8,128)(2,1)} %copy-done.13, bf16[4,128,512]{2,1,0:T(8,128)(2,1)} %copy-done.36, bf16[4,128,512]{2,1,0:T(8,128)(2,1)} %copy-done.37, bf16[4,128,512]{2,1,0:T(8,128)(2,1)} %copy-done.38), custom_call_target="tpu_custom_call" | custom-call | flops 4000000000 | bytes 40000 | tf_op jit(solution)/shard_map/place_feed/pallas_call | solution.py:913
  337.9 7.2 %collective-permute-done.51.other_ref = bf16[4,144,512]{2,1,0:T(8,128)(2,1)S(1)} collective-permute-done((bf16[4,144,512]{2,1,0:T(8,128)(2,1)S(1)}, bf16[4,144,512]{2,1,0:T(8,128)(2,1)S(1)}, u32[]{:S(2)}, u32[]{:S(2)}) %collective-permute-start.51) | collective-permute-done | bytes 589856 | tf_op jit(solution)/shard_map/ppermute | solution.py:933
  351.5 3.7 %place_maps.1 = (f32[6,256,512]{2,1,0:T(8,128)}, f32[2,256,512]{2,1,0:T(8,128)}, f32[3,256]{1,0:T(4,128)}, f32[10,256]{1,0:T(8,128)}, f32[4,256]{1,0:T(4,128)}) custom-call(s32[8,256]{1,0:T(8,128)} %copy-done.18, bf16[4,144,512]{2,1,0:T(8,128)(2,1)} %copy-done.8, bf16[4,144,512]{2,1,0:T(8,128)(2,1)} %copy-done.28, bf16[4,144,512]{2,1,0:T(8,128)(2,1)} %copy-done.29, ...), custom_call_target="tpu_custom_call" | custom-call | flops 4000000000 | bytes 40000 | tf_op jit(solution)/shard_map/place_maps/pallas_call | solution.py:913
  (265 shorter events, 118.4 us)
Async XLA Ops:
  7.2 93.4 %all-gather.3.cloned.1.call-start = ((), (), s32[]{:S(2)}) async-start(), calls=%async_computation.2 | async-start | bytes 2228224 | tf_op jit(solution)/shard_map/all_gather | solution.py:1089
  7.2 36.5 %collective-permute-start.7 = (bf16[256,512]{1,0:T(8,128)(2,1)}, bf16[256,512]{1,0:T(8,128)(2,1)S(1)}, u32[]{:S(2)}, u32[]{:S(2)}) collective-permute-start(bf16[256,512]{1,0:T(8,128)(2,1)} %bitcast.138), channel_id=1, source_target_pairs={{0,24},{2,26},{4,28},{6,30},{8,16},{10,18},{12,20},{14,22},{16,8},... | collective-permute-start | bytes 786440 | tf_op jit(solution)/shard_map/ppermute | solution.py:933
  8.6 43.2 %collective-permute-start.6 = (bf16[256,512]{1,0:T(8,128)(2,1)}, bf16[256,512]{1,0:T(8,128)(2,1)}, u32[]{:S(2)}, u32[]{:S(2)}) collective-permute-start(bf16[256,512]{1,0:T(8,128)(2,1)} %bitcast.139), channel_id=1, source_target_pairs={{0,16},{2,18},{4,20},{6,22},{8,24},{10,26},{12,28},{14,30},{16,0},... | collective-permute-start | bytes 786440 | tf_op jit(solution)/shard_map/ppermute | solution.py:933
  9.7 25.5 %collective-permute-start = (bf16[256,512]{1,0:T(8,128)(2,1)}, bf16[256,512]{1,0:T(8,128)(2,1)}, u32[]{:S(2)}, u32[]{:S(2)}) collective-permute-start(bf16[256,512]{1,0:T(8,128)(2,1)} %bitcast.140), channel_id=1, source_target_pairs={{0,8},{2,10},{4,12},{6,14},{8,0},{10,2},{12,4},{14,6},{16,24},{18,... | collective-permute-start | bytes 786440 | tf_op jit(solution)/shard_map/ppermute | solution.py:933
  10.8 337.4 %reduce-scatter.2.cloned.1.call-start = ((), (), s32[]{:S(2)}) async-start(), calls=%async_computation.1 | async-start | bytes 2228224 | tf_op jit(solution)/shard_map/reduce_scatter | solution.py:1253
  18.0 33.3 %collective-permute-start.3 = (bf16[400,512]{1,0:T(8,128)(2,1)}, bf16[400,512]{1,0:T(8,128)(2,1)}, u32[]{:S(2)}, u32[]{:S(2)}) collective-permute-start(bf16[400,512]{1,0:T(8,128)(2,1)} %pad_maximum_fusion.7), channel_id=1, source_target_pairs={{0,1},{1,0},{2,3},{3,2},{4,5},{5,4},{6,7},{7,6},{8,9},{9,8},{10,11... | collective-permute-start | bytes 1228808 | tf_op jit(solution)/shard_map/ppermute | solution.py:937
  36.9 27.2 %collective-permute-start.4 = (bf16[2,256,512]{2,1,0:T(8,128)(2,1)S(1)}, bf16[2,256,512]{2,1,0:T(8,128)(2,1)}, u32[]{:S(2)}, u32[]{:S(2)}) collective-permute-start(bf16[2,256,512]{2,1,0:T(8,128)(2,1)S(1)} %pad_maximum_fusion.4.refs_7_.refs_3_), channel_id=1, source_target_pairs={{0,4},{2,6},{4,0},{6,2},{8,12},{10,14},{12,8},{14,10},{16,20},{18,... | collective-permute-start | bytes 1572872 | tf_op jit(solution)/shard_map/ppermute | solution.py:933
  38.9 16.5 %collective-permute-start.1 = (bf16[2,128,512]{2,1,0:T(8,128)(2,1)}, bf16[2,128,512]{2,1,0:T(8,128)(2,1)S(1)}, u32[]{:S(2)}, u32[]{:S(2)}) collective-permute-start(bf16[2,128,512]{2,1,0:T(8,128)(2,1)} %get-tuple-element.215), channel_id=1, source_target_pairs={{0,0},{2,4},{4,8},{6,12},{8,16},{10,20},{12,24},{14,28},{16,30},{1... | collective-permute-start | bytes 786440 | tf_op jit(solution)/shard_map/ppermute | solution.py:1078
  43.7 18.4 %collective-permute-start.2 = (bf16[2,128,512]{2,1,0:T(8,128)(2,1)S(1)}, bf16[2,128,512]{2,1,0:T(8,128)(2,1)}, u32[]{:S(2)}, u32[]{:S(2)}) collective-permute-start(bf16[2,128,512]{2,1,0:T(8,128)(2,1)S(1)} %get-tuple-element.216), channel_id=1, source_target_pairs={{0,2},{2,6},{4,10},{6,14},{8,18},{10,22},{12,26},{14,30},{16,28},{... | collective-permute-start | bytes 786440 | tf_op jit(solution)/shard_map/ppermute | solution.py:1079
  51.3 14.9 %collective-permute-start.8 = (bf16[2,256,512]{2,1,0:T(8,128)(2,1)S(1)}, bf16[2,256,512]{2,1,0:T(8,128)(2,1)S(1)}, u32[]{:S(2)}, u32[]{:S(2)}) collective-permute-start(bf16[2,256,512]{2,1,0:T(8,128)(2,1)S(1)} %pad_maximum_fusion.4.refs_7_.refs_3_), channel_id=1, source_target_pairs={{0,2},{2,0},{4,6},{6,4},{8,10},{10,8},{12,14},{14,12},{16,18},{18,... | collective-permute-start | bytes 1572872 | tf_op jit(solution)/shard_map/ppermute | solution.py:933
  52.8 29.5 %collective-permute-start.10 = (bf16[2,256,512]{2,1,0:T(8,128)(2,1)S(1)}, bf16[2,256,512]{2,1,0:T(8,128)(2,1)S(1)}, u32[]{:S(2)}, u32[]{:S(2)}) collective-permute-start(bf16[2,256,512]{2,1,0:T(8,128)(2,1)S(1)} %pad_maximum_fusion.5.refs_8_.refs_7_), channel_id=1, source_target_pairs={{0,4},{2,6},{4,0},{6,2},{8,12},{10,14},{12,8},{14,10},{16,20},{18,... | collective-permute-start | bytes 1572872 | tf_op jit(solution)/shard_map/ppermute | solution.py:933
  55.5 41.3 %collective-permute-start.13 = (bf16[1664,512]{1,0:T(8,128)(2,1)}, bf16[1664,512]{1,0:T(8,128)(2,1)}, u32[]{:S(2)}, u32[]{:S(2)}) collective-permute-start(bf16[1664,512]{1,0:T(8,128)(2,1)} %slice_dynamic-update-slice_fusion), channel_id=1, source_target_pairs={{0,1},{1,0},{2,3},{3,2},{4,5},{5,4},{6,7},{7,6},{8,9},{9,8},{10,11... | collective-permute-start | bytes 5111816 | tf_op jit(solution)/shard_map/ppermute | solution.py:937
  123.3 29.4 %collective-permute-start.15 = (bf16[2,2,4,128,512]{4,3,2,1,0:T(8,128)(2,1)}, bf16[2,2,4,128,512]{4,3,2,1,0:T(8,128)(2,1)}, u32[]{:S(2)}, u32[]{:S(2)}) collective-permute-start(bf16[2,2,4,128,512]{4,3,2,1,0:T(8,128)(2,1)} %get-tuple-element.132), channel_id=1, source_target_pairs={{0,2},{2,0},{4,6},{6,4},{8,10},{10,8},{12,14},{14,12},{16,18},{18,... | collective-permute-start | bytes 6291464 | tf_op jit(solution)/shard_map/ppermute | solution.py:933
  138.7 46.2 %collective-permute-start.18 = (bf16[288,512]{1,0:T(8,128)(2,1)}, bf16[288,512]{1,0:T(8,128)(2,1)S(1)}, u32[]{:S(2)}, u32[]{:S(2)}) collective-permute-start(bf16[288,512]{1,0:T(8,128)(2,1)} %get-tuple-element.145.refs_2_), channel_id=1, source_target_pairs={{0,24},{2,26},{4,28},{6,30},{8,16},{10,18},{12,20},{14,22},{16,8},... | collective-permute-start | bytes 884744 | tf_op jit(solution)/shard_map/ppermute | solution.py:933
  143.5 41.3 %collective-permute-start.17 = (bf16[288,512]{1,0:T(8,128)(2,1)}, bf16[288,512]{1,0:T(8,128)(2,1)S(1)}, u32[]{:S(2)}, u32[]{:S(2)}) collective-permute-start(bf16[288,512]{1,0:T(8,128)(2,1)} %get-tuple-element.145.refs_2_), channel_id=1, source_target_pairs={{0,16},{2,18},{4,20},{6,22},{8,24},{10,26},{12,28},{14,30},{16,0},... | collective-permute-start | bytes 884744 | tf_op jit(solution)/shard_map/ppermute | solution.py:933
  166.8 19.0 %collective-permute-start.19 = (bf16[2,288,512]{2,1,0:T(8,128)(2,1)}, bf16[2,288,512]{2,1,0:T(8,128)(2,1)}, u32[]{:S(2)}, u32[]{:S(2)}) collective-permute-start(bf16[2,288,512]{2,1,0:T(8,128)(2,1)} %pad_maximum_fusion.1.refs_4_), channel_id=1, source_target_pairs={{0,4},{2,6},{4,0},{6,2},{8,12},{10,14},{12,8},{14,10},{16,20},{18,... | collective-permute-start | bytes 1769480 | tf_op jit(solution)/shard_map/ppermute | solution.py:933
  166.8 25.1 %collective-permute-start.21 = (bf16[2,4,128,512]{3,2,1,0:T(8,128)(2,1)S(1)}, bf16[2,4,128,512]{3,2,1,0:T(8,128)(2,1)}, u32[]{:S(2)}, u32[]{:S(2)}) collective-permute-start(bf16[2,4,128,512]{3,2,1,0:T(8,128)(2,1)S(1)} %fusion), channel_id=1, source_target_pairs={{0,1},{1,0},{2,3},{3,2},{4,5},{5,4},{6,7},{7,6},{8,9},{9,8},{10,11... | collective-permute-start | bytes 3145736 | tf_op jit(solution)/shard_map/ppermute | solution.py:937
  200.9 34.0 %collective-permute-start.20 = (bf16[2,2,4,112,512]{4,3,2,1,0:T(8,128)(2,1)}, bf16[2,2,4,112,512]{4,3,2,1,0:T(8,128)(2,1)S(1)}, u32[]{:S(2)}, u32[]{:S(2)}) collective-permute-start(bf16[2,2,4,112,512]{4,3,2,1,0:T(8,128)(2,1)} %get-tuple-element.164), channel_id=1, source_target_pairs={{0,2},{2,0},{4,6},{6,4},{8,10},{10,8},{12,14},{14,12},{16,18},{18,... | collective-permute-start | bytes 5505032 | tf_op jit(solution)/shard_map/ppermute | solution.py:933
  201.2 19.7 %collective-permute-start.25 = (bf16[2,288,512]{2,1,0:T(8,128)(2,1)}, bf16[2,288,512]{2,1,0:T(8,128)(2,1)S(1)}, u32[]{:S(2)}, u32[]{:S(2)}) collective-permute-start(bf16[2,288,512]{2,1,0:T(8,128)(2,1)} %pad_maximum_fusion.2.refs_6_), channel_id=1, source_target_pairs={{0,4},{2,6},{4,0},{6,2},{8,12},{10,14},{12,8},{14,10},{16,20},{18,... | collective-permute-start | bytes 1769480 | tf_op jit(solution)/shard_map/ppermute | solution.py:933
  213.4 22.9 %collective-permute-start.22 = (bf16[2,288,512]{2,1,0:T(8,128)(2,1)}, bf16[2,288,512]{2,1,0:T(8,128)(2,1)}, u32[]{:S(2)}, u32[]{:S(2)}) collective-permute-start(bf16[2,288,512]{2,1,0:T(8,128)(2,1)} %pad_maximum_fusion.1.refs_4_), channel_id=1, source_target_pairs={{0,2},{2,0},{4,6},{6,4},{8,10},{10,8},{12,14},{14,12},{16,18},{18,... | collective-permute-start | bytes 1769480 | tf_op jit(solution)/shard_map/ppermute | solution.py:933
  215.7 20.6 %collective-permute-start.23 = (bf16[2,288,512]{2,1,0:T(8,128)(2,1)}, bf16[2,288,512]{2,1,0:T(8,128)(2,1)}, u32[]{:S(2)}, u32[]{:S(2)}) collective-permute-start(bf16[2,288,512]{2,1,0:T(8,128)(2,1)} %collective-permute-done.19.refs_5_), channel_id=1, source_target_pairs={{0,2},{2,0},{4,6},{6,4},{8,10},{10,8},{12,14},{14,12},{16,18},{18,... | collective-permute-start | bytes 1769480 | tf_op jit(solution)/shard_map/ppermute | solution.py:933
  231.9 17.7 %collective-permute-start.26 = (bf16[2,288,512]{2,1,0:T(8,128)(2,1)}, bf16[2,288,512]{2,1,0:T(8,128)(2,1)}, u32[]{:S(2)}, u32[]{:S(2)}) collective-permute-start(bf16[2,288,512]{2,1,0:T(8,128)(2,1)} %pad_maximum_fusion.2.refs_6_), channel_id=1, source_target_pairs={{0,2},{2,0},{4,6},{6,4},{8,10},{10,8},{12,14},{14,12},{16,18},{18,... | collective-permute-start | bytes 1769480 | tf_op jit(solution)/shard_map/ppermute | solution.py:933
  233.7 16.0 %collective-permute-start.27 = (bf16[2,288,512]{2,1,0:T(8,128)(2,1)}, bf16[2,288,512]{2,1,0:T(8,128)(2,1)}, u32[]{:S(2)}, u32[]{:S(2)}) collective-permute-start(bf16[2,288,512]{2,1,0:T(8,128)(2,1)} %copy-done.27), channel_id=1, source_target_pairs={{0,2},{2,0},{4,6},{6,4},{8,10},{10,8},{12,14},{14,12},{16,18},{18,... | collective-permute-start | bytes 1769480 | tf_op jit(solution)/shard_map/ppermute | solution.py:933
  236.3 24.9 %collective-permute-start.31 = (bf16[2,4,112,512]{3,2,1,0:T(8,128)(2,1)}, bf16[2,4,112,512]{3,2,1,0:T(8,128)(2,1)}, u32[]{:S(2)}, u32[]{:S(2)}) collective-permute-start(bf16[2,4,112,512]{3,2,1,0:T(8,128)(2,1)} %fusion.2), channel_id=1, source_target_pairs={{0,1},{1,0},{2,3},{3,2},{4,5},{5,4},{6,7},{7,6},{8,9},{9,8},{10,11... | collective-permute-start | bytes 2752520 | tf_op jit(solution)/shard_map/ppermute | solution.py:937
  267.1 14.5 %collective-permute-start.38 = (bf16[2,2,4,32,512]{4,3,2,1,0:T(8,128)(2,1)}, bf16[2,2,4,32,512]{4,3,2,1,0:T(8,128)(2,1)S(1)}, u32[]{:S(2)}, u32[]{:S(2)}) collective-permute-start(bf16[2,2,4,32,512]{4,3,2,1,0:T(8,128)(2,1)} %get-tuple-element.179), channel_id=1, source_target_pairs={{0,2},{2,0},{4,6},{6,4},{8,10},{10,8},{12,14},{14,12},{16,18},{18,... | collective-permute-start | bytes 1572872 | tf_op jit(solution)/shard_map/ppermute | solution.py:933
  280.4 26.6 %collective-permute-start.47 = (bf16[4,128,512]{2,1,0:T(8,128)(2,1)S(1)}, bf16[4,128,512]{2,1,0:T(8,128)(2,1)S(1)}, u32[]{:S(2)}, u32[]{:S(2)}) collective-permute-start(bf16[4,128,512]{2,1,0:T(8,128)(2,1)S(1)} %pad_maximum_fusion.6.refs_1_), channel_id=1, source_target_pairs={{0,4},{2,6},{4,0},{6,2},{8,12},{10,14},{12,8},{14,10},{16,20},{18,... | collective-permute-start | bytes 1572872 | tf_op jit(solution)/shard_map/ppermute | solution.py:933
  309.4 16.2 %collective-permute-start.50 = (bf16[144,512]{1,0:T(8,128)(2,1)S(1)}, bf16[144,512]{1,0:T(8,128)(2,1)S(1)}, u32[]{:S(2)}, u32[]{:S(2)}) collective-permute-start(bf16[144,512]{1,0:T(8,128)(2,1)S(1)} %get-tuple-element.221), channel_id=1, source_target_pairs={{0,24},{2,26},{4,28},{6,30},{8,16},{10,18},{12,20},{14,22},{16,8},... | collective-permute-start | bytes 442376 | tf_op jit(solution)/shard_map/ppermute | solution.py:933
  309.8 21.4 %collective-permute-start.52 = (bf16[4,128,512]{2,1,0:T(8,128)(2,1)S(1)}, bf16[4,128,512]{2,1,0:T(8,128)(2,1)S(1)}, u32[]{:S(2)}, u32[]{:S(2)}) collective-permute-start(bf16[4,128,512]{2,1,0:T(8,128)(2,1)S(1)} %pad_maximum_fusion.6.refs_1_), channel_id=1, source_target_pairs={{0,2},{2,0},{4,6},{6,4},{8,10},{10,8},{12,14},{14,12},{16,18},{18,... | collective-permute-start | bytes 1572872 | tf_op jit(solution)/shard_map/ppermute | solution.py:933
  312.1 19.2 %collective-permute-start.53 = (bf16[4,128,512]{2,1,0:T(8,128)(2,1)S(1)}, bf16[4,128,512]{2,1,0:T(8,128)(2,1)S(1)}, u32[]{:S(2)}, u32[]{:S(2)}) collective-permute-start(bf16[4,128,512]{2,1,0:T(8,128)(2,1)S(1)} %collective-permute-done.47.refs_2_), channel_id=1, source_target_pairs={{0,2},{2,0},{4,6},{6,4},{8,10},{10,8},{12,14},{14,12},{16,18},{18,... | collective-permute-start | bytes 1572872 | tf_op jit(solution)/shard_map/ppermute | solution.py:933
  325.6 19.5 %collective-permute-start.51 = (bf16[4,144,512]{2,1,0:T(8,128)(2,1)S(1)}, bf16[4,144,512]{2,1,0:T(8,128)(2,1)S(1)}, u32[]{:S(2)}, u32[]{:S(2)}) collective-permute-start(bf16[4,144,512]{2,1,0:T(8,128)(2,1)S(1)} %pad_maximum_fusion.3.own_ref), channel_id=1, source_target_pairs={{0,4},{2,6},{4,0},{6,2},{8,12},{10,14},{12,8},{14,10},{16,20},{18,... | collective-permute-start | bytes 1769480 | tf_op jit(solution)/shard_map/ppermute | solution.py:933
  326.9 20.2 %collective-permute-start.32 = (bf16[2,128,512]{2,1,0:T(8,128)(2,1)S(1)}, bf16[2,128,512]{2,1,0:T(8,128)(2,1)S(1)}, u32[]{:S(2)}, u32[]{:S(2)}) collective-permute-start(bf16[2,128,512]{2,1,0:T(8,128)(2,1)S(1)} %get-tuple-element.208), channel_id=1, source_target_pairs={{0,0},{4,2},{8,4},{12,6},{16,8},{20,10},{24,12},{28,14},{30,16},{2... | collective-permute-start | bytes 786440 | tf_op jit(solution)/shard_map/ppermute | solution.py:1306
  328.8 18.2 %collective-permute-start.33 = (bf16[2,128,512]{2,1,0:T(8,128)(2,1)S(1)}, bf16[2,128,512]{2,1,0:T(8,128)(2,1)S(1)}, u32[]{:S(2)}, u32[]{:S(2)}) collective-permute-start(bf16[2,128,512]{2,1,0:T(8,128)(2,1)S(1)} %get-tuple-element.209), channel_id=1, source_target_pairs={{2,0},{6,2},{10,4},{14,6},{18,8},{22,10},{26,12},{30,14},{28,16},{... | collective-permute-start | bytes 786440 | tf_op jit(solution)/shard_map/ppermute | solution.py:1306
  (65 other events, 582.6 us)
Sparse Core Ops, SparseCore 0:
  10.9 53.2 all-gather.2
  271.7 63.9 reduce-scatter.1
where the time goes:
time: 366 us; the launch traced here: 364 us
  Pallas kernels  136 us (37%)
  starting transfers between devices  76.8 us (21%)
  waiting for transfers between devices  73.2 us (20%)
  other arithmetic  34.8 us (10%)
  local copies, waits for them, and re-layouts  28.1 us (8%)
  between operations  15.2 us (4%)
    pallas_call x14, Pallas kernels, call_kernel(): pl.pallas_call(kernel, in_specs=[smem] + [pl.BlockSpec(memory_space=pl.AN...  136 us
    ppermute x47, starting transfers between devices, exchange(): return lax.ppermute(value, 'ctx', [(i, i ^ bits) for i in range(count)])  63.1 us
    ppermute x47, waiting for transfers between devices, exchange(): return lax.ppermute(value, 'ctx', [(i, i ^ bits) for i in range(count)])  60.6 us
    unnamed x87, local copies, waits for them, and re-layouts  15.6 us
  transfers between devices with their start and end apart: 58, of which 20 were waited for; matrix products, arithmetic and copies ran while one was open for 13% of the time, Pallas kernels for 29%

commit v1 on v0

--- a/solution.py
+++ b/solution.py
@@ -139,13 +139,16 @@
         base = pl.multiple_of(stored * key_rows, key_rows)
         key_pos = index * key_rows + lax.broadcasted_iota(jnp.int32, (1, key_rows), 1)
         allowed = (key_pos >= low2) & (key_pos <= high2)
+        def read(pair, offset):
+            start = offset + pair * tile_width
+            return kv_ref[pl.ds(base, key_rows), start : start + tile_width]
+
+        scores = [dot_nt(stacked[0], read(0, 0))]
         for pair in range(PAIRS):
-            start = pair * tile_width
-            keys = kv_ref[pl.ds(base, key_rows), start : start + tile_width]
-            values = kv_ref[pl.ds(base, key_rows), width + start : width + start + tile_width]
-            scores = dot_nt(stacked[pair], keys)
-            weights = jnp.where(allowed, jnp.exp2(scores * factor), 0.0).astype(bf16)
-            acc_ref[pair] += dot_nn(weights, jnp.concatenate([values, ones], axis=1))
+            if pair + 1 < PAIRS:
+                scores.append(dot_nt(stacked[pair + 1], read(pair + 1, 0)))
+            weights = jnp.where(allowed, jnp.exp2(scores[pair] * factor), 0.0).astype(bf16)
+            acc_ref[pair] += dot_nn(weights, jnp.concatenate([read(pair, width), ones], axis=1))
 
     run(step)
 
@@ -214,18 +217,24 @@
         base = pl.multiple_of(stored * key_rows, key_rows)
         key_pos = index * key_rows + lax.broadcasted_iota(jnp.int32, (1, key_rows), 1)
         allowed = (key_pos >= low2) & (key_pos <= high2)
+        def read(pair, offset):
+            start = offset + pair * tile_width
+            return kv_ref[pl.ds(base, key_rows), start : start + tile_width]
+
+        def products(pair):
+            return dot_nt(q2[pair], read(pair, 0)), dot_nt(g2[pair], read(pair, width))
+
+        ahead = products(0)
+        repeats = key_rows // log_ref.shape[2]
         for pair in range(PAIRS):
-            start = pair * tile_width
-            keys = kv_ref[pl.ds(base, key_rows), start : start + tile_width]
-            values = kv_ref[pl.ds(base, key_rows), width + start : width + start + tile_width]
-            scores = dot_nt(q2[pair], keys)
-            repeats = key_rows // log_ref.shape[2]
+            scores, prob_grad = ahead
+            if pair + 1 < PAIRS:
+                ahead = products(pair + 1)
             logs = jnp.concatenate([log_ref[pair]] * repeats, axis=1)
             deltas = jnp.concatenate([delta_ref[pair]] * repeats, axis=1)
             probs = jnp.where(allowed, jnp.exp2(scores * factor - logs), 0.0)
-            prob_grad = dot_nt(g2[pair], values)
             score_grad = (probs * (prob_grad - deltas)).astype(bf16)
-            acc_ref[pair] += dot_nn(score_grad, keys)
+            acc_ref[pair] += dot_nn(score_grad, read(pair, 0))
 
     run(step)
 
@@ -255,16 +264,21 @@
                 axis=0,
             )
 
+        def read(ref, start, pair):
+            return ref[pl.ds(start, query_rows), pair * tile_width : (pair + 1) * tile_width]
+
+        def products(pair):
+            return dot_nt(k2[pair], read(q_ref, q_base, pair)), dot_nt(v2[pair], read(g_ref, base, pair))
+
+        ahead = products(0)
         for pair in range(PAIRS):
-            lanes = slice(pair * tile_width, (pair + 1) * tile_width)
-            queries = q_ref[pl.ds(q_base, query_rows), lanes]
-            upstream = g_ref[pl.ds(base, query_rows), lanes]
-            scores = dot_nt(k2[pair], queries)
+            scores, prob_grad = ahead
+            if pair + 1 < PAIRS:
+                ahead = products(pair + 1)
             probs = jnp.where(allowed, jnp.exp2(scores * factor - two_rows(2 * pair)), 0.0)
-            prob_grad = dot_nt(v2[pair], upstream)
             score_grad = (probs * (prob_grad - two_rows(HEADS + 2 * pair))).astype(bf16)
-            dk_ref[pair] += dot_nn(score_grad, queries)
-            dv_ref[pair] += dot_nn(probs.astype(bf16), upstream)
+            dk_ref[pair] += dot_nn(score_grad, read(q_ref, q_base, pair))
+            dv_ref[pair] += dot_nn(probs.astype(bf16), read(g_ref, base, pair))
 
     run(step)
 
@@ -430,15 +444,23 @@
     return jnp.sum(matrix.astype(f32), axis=0, keepdims=True)
 
 
+def piece_rows(pieces):
+    for bits in range(4):
+        ref = pieces[(bits >> 1) + 2 * (bits & 1)]
+        yield bits, ref[...].reshape(ref.shape[0] * ref.shape[1], ref.shape[2])
+
+
 def project_chunks(pieces, planes, kv_ref, w_ref, shift, info):
     width = w_ref.shape[2]
     rows = pieces[0].shape[1]
-    for s, bits, chunk in chunk_views(pieces, planes):
-        start = 4 * rows * s + rows * ((info.me & 3) ^ bits)
-        at = pl.ds(pl.multiple_of(start, rows), rows)
-        block = chunk[...]
-        kv_ref[at, 0:width] = dot_nn(block, w_ref[1]).astype(bf16)
-        kv_ref[at, width:] = (dot_nn(block, w_ref[2]) + shift).astype(bf16)
+    for bits, block in piece_rows(pieces):
+        keys = dot_nn(block, w_ref[1]).astype(bf16)
+        values = (dot_nn(block, w_ref[2]) + shift).astype(bf16)
+        for s in range(planes):
+            start = 4 * rows * s + rows * ((info.me & 3) ^ bits)
+            at = pl.ds(pl.multiple_of(start, rows), rows)
+            kv_ref[at, 0:width] = keys[s * rows : (s + 1) * rows]
+            kv_ref[at, width:] = values[s * rows : (s + 1) * rows]
 
 
 def first_forward_kernel(info_ref, x_ref, bias_ref, cols_ref, *refs, factor, planes, shards):
@@ -517,11 +539,13 @@
     pieces, (q_ref,) = refs[:8], refs[8:]
     info = RowInfo(info_ref)
     for part in range(2):
-        for s, bits, chunk in chunk_views(pieces[4 * part : 4 * part + 4], planes):
-            rows = chunk.shape[0]
-            place = info.me ^ (4 * (part * planes + s) + bits)
-            at = pl.ds(pl.multiple_of(place * rows, rows), rows)
-            q_ref[at, :] = (dot_nn(chunk[...], w_ref[0]) + bias_ref[0:1, :]).astype(bf16)
+        for bits, block in piece_rows(pieces[4 * part : 4 * part + 4]):
+            queries = (dot_nn(block, w_ref[0]) + bias_ref[0:1, :]).astype(bf16)
+            rows = pieces[0].shape[1]
+            for s in range(planes):
+                place = info.me ^ (4 * (part * planes + s) + bits)
+                at = pl.ds(pl.multiple_of(place * rows, rows), rows)
+                q_ref[at, :] = queries[s * rows : (s + 1) * rows]
 
 
 def middle_forward_kernel(
@@ -852,6 +876,14 @@
     put_small(sink, 6, dw_ref, sums_ref[...], csum_ref, dq_ref[...])
 
 
+def grads_project_kernel(info_ref, w_ref, bias_ref, *refs, planes, plain):
+    pieces, refs = refs[:8], refs[8:]
+    inputs, refs = refs[:11], refs[11:]
+    q_ref, outs = refs[0], refs[1:]
+    map_grads_kernel(info_ref, *inputs, *outs, plain=plain)
+    project_kernel(info_ref, w_ref, bias_ref, *pieces, q_ref, planes=planes)
+
+
 def put_small(sink, block, dw_ref, sums, csum_ref, dq):
     dw_ref[...] = jnp.zeros(dw_ref.shape, f32)
     row = lax.broadcasted_iota(jnp.int32, sums.shape, 0)
@@ -941,9 +973,8 @@
     return lax.optimization_barrier((value,) + others)[0]
 
 
-def fetch_planes(value):
-    planes = lax.axis_size("ctx") // 4
-    return [value] + [exchange(value, 4 * s) for s in range(1, planes)]
+def fetch_planes(value, first, last):
+    return [exchange(value, 4 * s) if s else value for s in range(first, last)]
 
 
 def fetch_chips(chunks):
@@ -1025,7 +1056,7 @@
     mem_total = mem_count * count
     near, far = planes // 2, planes - planes // 2
 
-    x_planes = fetch_planes(tokens[0])
+    x_planes = fetch_planes(tokens[0], 0, planes)
     small = jnp.concatenate(
         [norm_gain, bias_rows, ffn_bias.reshape(-1, norm_gain.shape[1])], axis=0
     ).astype(bf16)
@@ -1205,7 +1236,7 @@
         "middle_backward",
         14,
     )
-    g_planes = fetch_planes(ga)
+    g_planes = fetch_planes(ga, 0, near)
     if not plain:
         feed = add_cores(*feed)
         dkvc = after(dkvc, feed[1])
@@ -1217,7 +1248,8 @@
         "memory_grads",
         5,
     )
-    g_near = fetch_chips(jnp.stack([after(chunk, mem_part) for chunk in g_planes[:near]]))
+    g_near = fetch_chips(jnp.stack([after(chunk, mem_part) for chunk in g_planes]))
+    g_planes = fetch_planes(after(ga, mem_part), near, planes)
     (dq,) = call_kernel(
         lambda *refs: query_backward_kernel(*refs, factor=factor, scale=scale, planes=near),
         (info, after(q_rows, g_near[0]), ga, kv_near, kv_far, log_rows, delta, cols),
@@ -1226,28 +1258,26 @@
         "query_backward",
         20,
     )
-    g_far = fetch_chips(jnp.stack([after(chunk, dq) for chunk in g_planes[near:]]))
+    g_far = fetch_chips(jnp.stack([after(chunk, dq) for chunk in g_planes]))
     g_near = fetch_cores([after(chunks, dq) for chunks in g_near])
-    maps = call_kernel(
-        lambda *refs: map_grads_kernel(*refs, plain=plain),
-        (info, a_low, e1, ac_low, e2, after(h1_low, g_far[0], g_near[1]), dqc, dwc, x_rows, dq, sums, csum),
-        sink_shapes(7),
+    if not plain:
+        feed = add_sides(*feed)
+        feed_low = feed[1].astype(bf16)
+        h1_low = after(h1_low, feed_low)
+    q_all, *maps = call_kernel(
+        lambda *refs: grads_project_kernel(*refs, planes=near, plain=plain),
+        (
+            info, w_self, biases, *x_near, *x_far, a_low, e1, ac_low, e2,
+            after(h1_low, g_far[0], g_near[1]), dqc, dwc, x_rows, dq, sums, csum,
+        ),
+        [((total, width), bf16)] + sink_shapes(7),
         [((width, width), f32)],
-        "map_grads",
-        6,
-    )
-    (q_all,) = call_kernel(
-        lambda *refs: project_kernel(*refs, planes=near),
-        (info, after(w_self, maps[0]), biases, *x_near, *x_far),
-        (((total, width), bf16),),
-        [],
-        "project",
-        7,
+        "grads_project",
+        12,
     )
     if not plain:
         maps = add_cores(*maps)
-        feed = add_sides(*feed)
-        feed_low = feed[1].astype(bf16)
+        feed_low = after(feed_low, q_all)
         kv_rows = after(kv_rows, maps[1], feed_low)
     mem_part = after(mem_part, g_far[1])
     memory_grad = lax.psum_scatter(mem_part, "ctx", scatter_dimension=0, tiled=True).astype(f32)
@@ -1266,7 +1296,7 @@
         8,
     )
     if not plain:
-        feed = add_chips(feed, feed_low)
+        feed = feed[0] + after(exchange(feed_low, 2), dk_part).astype(f32)
         feed_low = low_planes(feed)
         dk_part = after(dk_part, *feed_low)
     dk, dv = call_kernel(
@@ -1280,7 +1310,7 @@
             two_squares, two_squares,
         ],
         "key_backward_last",
-        12,
+        3,
     )
     if not plain:
         feed = add_planes(feed, feed_low).astype(bf16)

time: 366 us -> 357 us (0.975)
  Pallas kernels: 136 us -> 129 us
    ppermute x47, starting transfers between devices: 63.1 us -> 55 us  [exchange(): return lax.ppermute(value, 'ctx', [(i, i ^ bits) for i in range(count)])]
    pallas_call x14 -> x13, Pallas kernels: 136 us -> 129 us  [call_kernel(): pl.pallas_call(kernel, in_specs=[smem] + [pl.BlockSpec(memory_space=pl.AN...]
    ppermute x5, waiting for transfers between devices: 6.17 us -> 0.01 us  [swap_side(): return lax.ppermute(value, 'fsdp', [(0, 1), (1, 0)])]
    ppermute x47, waiting for transfers between devices: 60.6 us -> 65.2 us  [exchange(): return lax.ppermute(value, 'ctx', [(i, i ^ bits) for i in range(count)])]
    ppermute x5, starting transfers between devices: 2.41 us -> 6.85 us  [swap_side(): return lax.ppermute(value, 'fsdp', [(0, 1), (1, 0)])]
    unnamed x87 -> x89, local copies, waits for them, and re-layouts: 15.6 us -> 17.5 us
  transfers between devices with their start and end apart: 58 -> 58, of which waited for: 20 -> 20; matrix products, arithmetic and copies ran while one was open for 13% -> 13% of each run, Pallas kernels for 29% -> 26%
where the time goes in v1:
time: 357 us; the launch traced here: 352 us
  Pallas kernels  129 us (36%)
  starting transfers between devices  73.4 us (21%)
  waiting for transfers between devices  71.6 us (20%)
  other arithmetic  33.5 us (9%)
  local copies, waits for them, and re-layouts  29.2 us (8%)
  between operations  15.2 us (4%)
    pallas_call x13, Pallas kernels, call_kernel(): pl.pallas_call(kernel, in_specs=[smem] + [pl.BlockSpec(memory_space=pl.AN...  129 us
    ppermute x47, waiting for transfers between devices, exchange(): return lax.ppermute(value, 'ctx', [(i, i ^ bits) for i in range(count)])  65.2 us
    ppermute x47, starting transfers between devices, exchange(): return lax.ppermute(value, 'ctx', [(i, i ^ bits) for i in range(count)])  55 us
    unnamed x89, local copies, waits for them, and re-layouts  17.5 us
  transfers between devices with their start and end apart: 58, of which 20 were waited for; matrix products, arithmetic and copies ran while one was open for 13% of the time, Pallas kernels for 26%

profile of v1, /device:TPU:9, one launch (start us, length us, event | category | flops | bytes accessed | tf_op | source)
XLA Modules:
  0.0 351.7 jit_solution(6770181955173914334)
XLA Ops:
  13.0 3.0 fusion.37
  28.3 2.6 fusion.4
  39.0 4.7 %collective-permute-start.1 = (bf16[2,128,512]{2,1,0:T(8,128)(2,1)}, bf16[2,128,512]{2,1,0:T(8,128)(2,1)S(1)}, u32[]{:S(2)}, u32[]{:S(2)}) collective-permute-start(bf16[2,128,512]{2,1,0:T(8,128)(2,1)} %get-tuple-element.221), channel_id=1, source_target_pairs={{0,0},{2,4},{4,8},{6,12},{8,16},{10,20},{12,24},{14,28},{16,30},{1... | collective-permute-start | bytes 786440 | tf_op jit(solution)/shard_map/ppermute | solution.py:1109
  52.8 2.7 collective-permute-start.10
  55.7 6.4 %collective-permute-done.2 = bf16[2,128,512]{2,1,0:T(8,128)(2,1)} collective-permute-done((bf16[2,128,512]{2,1,0:T(8,128)(2,1)}, bf16[2,128,512]{2,1,0:T(8,128)(2,1)}, u32[]{:S(2)}, u32[]{:S(2)}) %collective-permute-start.2) | collective-permute-done | bytes 262176 | tf_op jit(solution)/shard_map/ppermute | solution.py:1110
  68.5 13.3 %first_forward.1 = (bf16[256,512]{1,0:T(8,128)(2,1)}, bf16[256,1024]{1,0:T(8,128)(2,1)}, bf16[2048,1024]{1,0:T(8,128)(2,1)}, bf16[3,512,512]{2,1,0:T(8,128)(2,1)...) custom-call(s32[8,256]{1,0:T(8,128)} %copy-done.18, bf16[256,512]{1,0:T(8,128)(2,1)} %get-tuple-element.220.refs_1_.refs_18_, ...), custom_call_target="tpu_custom_call" | custom-call | flops 10000000000 | bytes 100000 | tf_op jit(solution)/shard_map/first_forward/pallas_call | solution.py:945
  85.3 10.8 %second_forward.1 = (f32[256,512]{1,0:T(8,128)}, f32[8,256]{1,0:T(8,128)}, bf16[2048,1024]{1,0:T(8,128)(2,1)}) custom-call(s32[8,256]{1,0:T(8,128)} %copy-done.18, bf16[2048,1024]{1,0:T(8,128)(2,1)} %get-tuple-element.112.refs_1_.refs_3_, bf16[256,512]{1,0:T(8,128)(2,1)} %get-tuple-element.150.refs_2_.refs_1_, f32[10,512]{1,0:T(8,128)} %bitcast.154, ...), custom_call_target="tpu_custom_call" | custom-call | flops 10000000000 | bytes 100000 | tf_op jit(solution)/shard_map/second_forward/pallas_call | solution.py:945
  101.2 15.9 %middle_forward.1 = (f32[256,512]{1,0:T(8,128)}, bf16[256,512]{1,0:T(8,128)(2,1)}, bf16[256,512]{1,0:T(8,128)(2,1)}, bf16[256,512]{1,0:T(8,128)(2,1)}, bf16[256,...) custom-call(s32[8,256]{1,0:T(8,128)} %copy-done.18, ...), custom_call_target="tpu_custom_call" | custom-call | flops 24999999488 | bytes 250000 | tf_op jit(solution)/shard_map/middle_forward/pallas_call | solution.py:945
  117.1 5.3 %feed_grads.1 = (bf16[2,2,4,128,512]{4,3,2,1,0:T(8,128)(2,1)}, bf16[2,2,4,128,512]{4,3,2,1,0:T(8,128)(2,1)}) custom-call(s32[8,256]{1,0:T(8,128)} %copy-done.18, bf16[256,512]{1,0:T(8,128)(2,1)} %get-tuple-element.130.refs_1_, bf16[256,2048]{1,0:T(8,128)(2,1)} %get-tuple-element.131.refs_2_, bf16[256,2048]{1,0:T(8,128)(2,1)} %get-tuple-element.132.refs_3_, ...), custom_call_target="tpu_custom_call" | custom-call | flops 5000000000 | bytes 50000 | tf_op jit(solution)/shard_map/feed_grads/pallas_call | solution.py:945
  122.8 15.1 %middle_backward.1 = (bf16[256,512]{1,0:T(8,128)(2,1)}, bf16[256,512]{1,0:T(8,128)(2,1)}, bf16[288,512]{1,0:T(8,128)(2,1)}, f32[256,512]{1,0:T(8,128)}, f32[8,25...) custom-call(s32[8,256]{1,0:T(8,128)} %copy-done.18, f32[256,512]{1,0:T(8,128)} %get-tuple-element.119.refs_2_.refs_1_, ...), custom_call_target="tpu_custom_call" | custom-call | flops 14000000000 | bytes 140000 | tf_op jit(solution)/shard_map/middle_backward/pallas_call | solution.py:945
  137.9 8.2 %collective-permute-start.16 = (bf16[288,512]{1,0:T(8,128)(2,1)}, bf16[288,512]{1,0:T(8,128)(2,1)S(1)}, u32[]{:S(2)}, u32[]{:S(2)}) collective-permute-start(bf16[288,512]{1,0:T(8,128)(2,1)} %get-tuple-element.148.refs_2_), channel_id=1, source_target_pairs={{0,8},{2,10},{4,12},{6,14},{8,0},{10,2},{12,4},{14,6},{16,24},{18,... | collective-permute-start | bytes 884744 | tf_op jit(solution)/shard_map/ppermute | solution.py:965
  147.7 7.8 %memory_grads.1 = (bf16[2048,512]{1,0:T(8,128)(2,1)}, bf16[512,1024]{1,0:T(8,128)(2,1)}) custom-call(s32[8,256]{1,0:T(8,128)} %copy-done.18, bf16[2048,512]{1,0:T(8,128)(2,1)} %bitcast.169, bf16[5,512,512]{2,1,0:T(8,128)(2,1)} %get-tuple-element.127.refs_5_.refs_2_, bf16[2048,1024]{1,0:T(8,128)(2,1)} %get-tuple-element.146.refs_3_), custom_call_target="tpu_custom_call" | custom-call | flops 5000000000 | bytes 50000 | tf_op jit(solution)/shard_map/memory_grads/pallas_call | solution.py:945
  158.5 3.0 collective-permute-start.17
  161.5 16.1 %query_backward.1.refs_19_.refs_3_ = bf16[256,512]{1,0:T(8,128)(2,1)} custom-call(s32[8,256]{1,0:T(8,128)} %copy-done.18, bf16[256,512]{1,0:T(8,128)(2,1)} %get-tuple-element.150.refs_2_.refs_1_, bf16[288,512]{1,0:T(8,128)(2,1)} %get-tuple-element.148.refs_2_, bf16[2048,1024]{1,0:T(8,128)(2,1)} %get-tuple-element.112.refs_1_.refs_3_, ...), custom_call_target="tpu_custom_call" | custom-call | flops 20000000000 | bytes 200000 | tf_op jit(solution)/shard_map/query_backward/pallas_call | solution.py:945
  177.6 3.4 collective-permute-done.18
  184.2 10.3 %grads_project.1 = (bf16[4096,512]{1,0:T(8,128)(2,1)}, bf16[2,2,4,112,512]{4,3,2,1,0:T(8,128)(2,1)}, bf16[2,2,4,112,512]{4,3,2,1,0:T(8,128)(2,1)}) custom-call(s32[8,256]{1,0:T(8,128)} %copy-done.18, bf16[3,512,512]{2,1,0:T(8,128)(2,1)} %get-tuple-element.114.refs_5_.refs_1_.refs_6_, f32[10,512]{1,0:T(8,128)} %bitcast.156, bf16[2,256,512]{2,1,0:T(8,128)(2,1)} %copy-done.10, ...), custom_call_target="tpu_custom_call" | custom-call | flops 12000000000 | bytes 120000 | tf_op jit(solution)/shard_map/grads_project/pallas_call | solution.py:945
  194.5 3.8 %collective-permute-start.21 = (bf16[2,2,4,112,512]{4,3,2,1,0:T(8,128)(2,1)}, bf16[2,2,4,112,512]{4,3,2,1,0:T(8,128)(2,1)S(1)}, u32[]{:S(2)}, u32[]{:S(2)}) collective-permute-start(bf16[2,2,4,112,512]{4,3,2,1,0:T(8,128)(2,1)} %get-tuple-element.168), channel_id=1, source_target_pairs={{0,2},{2,0},{4,6},{6,4},{8,10},{10,8},{12,14},{14,12},{16,18},{18,... | collective-permute-start | bytes 5505032 | tf_op jit(solution)/shard_map/ppermute | solution.py:965
  200.4 13.3 %collective-permute-done.25.refs_7_ = bf16[2,288,512]{2,1,0:T(8,128)(2,1)} collective-permute-done((bf16[2,288,512]{2,1,0:T(8,128)(2,1)}, bf16[2,288,512]{2,1,0:T(8,128)(2,1)}, u32[]{:S(2)}, u32[]{:S(2)}) %collective-permute-start.25) | collective-permute-done | bytes 589856 | tf_op jit(solution)/shard_map/ppermute | solution.py:965
  220.8 12.2 %key_backward.1 = (f32[2,4,256,128]{3,2,1,0:T(8,128)}, f32[2,4,256,128]{3,2,1,0:T(8,128)}) custom-call(s32[8,256]{1,0:T(8,128)} %copy-done.18, bf16[256,1024]{1,0:T(8,128)(2,1)} %get-tuple-element.171.refs_1_, bf16[4096,512]{1,0:T(8,128)(2,1)} %get-tuple-element.169.refs_2_, s32[256,8]{1,0:T(8,128)} %copy.30.refs_3_.refs_4_.refs_7_, ...), custom_call_target="tpu_custom_call" | custom-call | flops 8000000000 | bytes 80000 | tf_op jit(solution)/shard_map/key_backward/pallas_call | solution.py:945
  237.8 10.7 %key_backward_last.1 = (bf16[256,512]{1,0:T(8,128)(2,1)}, bf16[256,512]{1,0:T(8,128)(2,1)}) custom-call(s32[8,256]{1,0:T(8,128)} %copy-done.18, bf16[256,1024]{1,0:T(8,128)(2,1)} %get-tuple-element.171.refs_1_, bf16[4096,512]{1,0:T(8,128)(2,1)} %get-tuple-element.169.refs_2_, s32[256,8]{1,0:T(8,128)} %copy.30.refs_3_.refs_4_.refs_7_, ...), custom_call_target="tpu_custom_call" | custom-call | flops 3000000000 | bytes 30000 | tf_op jit(solution)/shard_map/key_backward_last/pallas_call | solution.py:945
  251.3 3.8 %self_grads.1 = (bf16[256,512]{1,0:T(8,128)(2,1)}, bf16[2,2,4,32,512]{4,3,2,1,0:T(8,128)(2,1)}, bf16[2,2,4,32,512]{4,3,2,1,0:T(8,128)(2,1)}) custom-call(s32[8,256]{1,0:T(8,128)} %copy-done.18, bf16[256,512]{1,0:T(8,128)(2,1)} %get-tuple-element.220.refs_1_.refs_18_, f32[256,512]{1,0:T(8,128)} %get-tuple-element.143.refs_2_, ...), custom_call_target="tpu_custom_call" | custom-call | flops 4000000000 | bytes 40000 | tf_op jit(solution)/shard_map/self_grads/pallas_call | solution.py:945
  259.2 8.1 %collective-permute-done.42 = bf16[128,512]{1,0:T(8,128)(2,1)S(1)} collective-permute-done((bf16[128,512]{1,0:T(8,128)(2,1)}, bf16[128,512]{1,0:T(8,128)(2,1)S(1)}, u32[]{:S(2)}, u32[]{:S(2)}) %collective-permute-start.42) | collective-permute-done | bytes 131104 | tf_op jit(solution)/shard_map/ppermute | solution.py:965
  271.4 3.0 collective-permute-start.35
  278.2 5.1 %collective-permute-done.37 = bf16[112,512]{1,0:T(8,128)(2,1)S(1)} collective-permute-done((bf16[112,512]{1,0:T(8,128)(2,1)S(1)}, bf16[112,512]{1,0:T(8,128)(2,1)S(1)}, u32[]{:S(2)}, u32[]{:S(2)}) %collective-permute-start.37) | collective-permute-done | bytes 114720 | tf_op jit(solution)/shard_map/ppermute | solution.py:965
  284.8 3.2 collective-permute-start.45
  290.7 4.3 %collective-permute-done.46 = bf16[32,512]{1,0:T(8,128)(2,1)S(1)} collective-permute-done((bf16[32,512]{1,0:T(8,128)(2,1)S(1)}, bf16[32,512]{1,0:T(8,128)(2,1)S(1)}, u32[]{:S(2)}, u32[]{:S(2)}) %collective-permute-start.46) | collective-permute-done | bytes 32800 | tf_op jit(solution)/shard_map/ppermute | solution.py:965
  299.9 5.3 %collective-permute-done.49 = bf16[144,512]{1,0:T(8,128)(2,1)S(1)} collective-permute-done((bf16[144,512]{1,0:T(8,128)(2,1)S(1)}, bf16[144,512]{1,0:T(8,128)(2,1)S(1)}, u32[]{:S(2)}, u32[]{:S(2)}) %collective-permute-start.49) | collective-permute-done | bytes 147488 | tf_op jit(solution)/shard_map/ppermute | solution.py:965
  306.7 6.8 %collective-permute-done.50 = bf16[144,512]{1,0:T(8,128)(2,1)S(1)} collective-permute-done((bf16[144,512]{1,0:T(8,128)(2,1)S(1)}, bf16[144,512]{1,0:T(8,128)(2,1)S(1)}, u32[]{:S(2)}, u32[]{:S(2)}) %collective-permute-start.50) | collective-permute-done | bytes 147488 | tf_op jit(solution)/shard_map/ppermute | solution.py:965
  316.5 2.6 collective-permute-start.33
  320.8 3.9 %place_feed.1 = (f32[256,2048]{1,0:T(8,128)}, f32[1024,512]{1,0:T(8,128)}) custom-call(s32[8,256]{1,0:T(8,128)} %copy-done.18, bf16[4,128,512]{2,1,0:T(8,128)(2,1)} %copy-done.12, bf16[4,128,512]{2,1,0:T(8,128)(2,1)} %copy-done.34, bf16[4,128,512]{2,1,0:T(8,128)(2,1)} %copy-done.37, bf16[4,128,512]{2,1,0:T(8,128)(2,1)} %copy-done.38), custom_call_target="tpu_custom_call" | custom-call | flops 4000000000 | bytes 40000 | tf_op jit(solution)/shard_map/place_feed/pallas_call | solution.py:945
  325.1 8.0 %collective-permute-done.51.other_ref = bf16[4,144,512]{2,1,0:T(8,128)(2,1)S(1)} collective-permute-done((bf16[4,144,512]{2,1,0:T(8,128)(2,1)S(1)}, bf16[4,144,512]{2,1,0:T(8,128)(2,1)S(1)}, u32[]{:S(2)}, u32[]{:S(2)}) %collective-permute-start.51) | collective-permute-done | bytes 589856 | tf_op jit(solution)/shard_map/ppermute | solution.py:965
  339.4 3.7 %place_maps.1 = (f32[6,256,512]{2,1,0:T(8,128)}, f32[2,256,512]{2,1,0:T(8,128)}, f32[3,256]{1,0:T(4,128)}, f32[10,256]{1,0:T(8,128)}, f32[4,256]{1,0:T(4,128)}) custom-call(s32[8,256]{1,0:T(8,128)} %copy-done.18, bf16[4,144,512]{2,1,0:T(8,128)(2,1)} %copy-done.7, bf16[4,144,512]{2,1,0:T(8,128)(2,1)} %copy-done.27, bf16[4,144,512]{2,1,0:T(8,128)(2,1)} %copy-done.28, ...), custom_call_target="tpu_custom_call" | custom-call | flops 4000000000 | bytes 40000 | tf_op jit(solution)/shard_map/place_maps/pallas_call | solution.py:945
  (266 shorter events, 110.2 us)
Async XLA Ops:
  7.2 92.8 %all-gather.3.cloned.1.call-start = ((), (), s32[]{:S(2)}) async-start(), calls=%async_computation.2 | async-start | bytes 2228224 | tf_op jit(solution)/shard_map/all_gather | solution.py:1120
  7.2 36.5 %collective-permute-start.7 = (bf16[256,512]{1,0:T(8,128)(2,1)}, bf16[256,512]{1,0:T(8,128)(2,1)S(1)}, u32[]{:S(2)}, u32[]{:S(2)}) collective-permute-start(bf16[256,512]{1,0:T(8,128)(2,1)} %bitcast.138), channel_id=1, source_target_pairs={{0,24},{2,26},{4,28},{6,30},{8,16},{10,18},{12,20},{14,22},{16,8},... | collective-permute-start | bytes 786440 | tf_op jit(solution)/shard_map/ppermute | solution.py:965
  8.6 43.2 %collective-permute-start.6 = (bf16[256,512]{1,0:T(8,128)(2,1)}, bf16[256,512]{1,0:T(8,128)(2,1)}, u32[]{:S(2)}, u32[]{:S(2)}) collective-permute-start(bf16[256,512]{1,0:T(8,128)(2,1)} %bitcast.139), channel_id=1, source_target_pairs={{0,16},{2,18},{4,20},{6,22},{8,24},{10,26},{12,28},{14,30},{16,0},... | collective-permute-start | bytes 786440 | tf_op jit(solution)/shard_map/ppermute | solution.py:965
  9.7 25.5 %collective-permute-start = (bf16[256,512]{1,0:T(8,128)(2,1)}, bf16[256,512]{1,0:T(8,128)(2,1)}, u32[]{:S(2)}, u32[]{:S(2)}) collective-permute-start(bf16[256,512]{1,0:T(8,128)(2,1)} %bitcast.140), channel_id=1, source_target_pairs={{0,8},{2,10},{4,12},{6,14},{8,0},{10,2},{12,4},{14,6},{16,24},{18,... | collective-permute-start | bytes 786440 | tf_op jit(solution)/shard_map/ppermute | solution.py:965
  10.8 324.2 %reduce-scatter.2.cloned.1.call-start = ((), (), s32[]{:S(2)}) async-start(), calls=%async_computation.1 | async-start | bytes 2228224 | tf_op jit(solution)/shard_map/reduce_scatter | solution.py:1283
  18.0 33.4 %collective-permute-start.3 = (bf16[400,512]{1,0:T(8,128)(2,1)}, bf16[400,512]{1,0:T(8,128)(2,1)}, u32[]{:S(2)}, u32[]{:S(2)}) collective-permute-start(bf16[400,512]{1,0:T(8,128)(2,1)} %pad_maximum_fusion.7), channel_id=1, source_target_pairs={{0,1},{1,0},{2,3},{3,2},{4,5},{5,4},{6,7},{7,6},{8,9},{9,8},{10,11... | collective-permute-start | bytes 1228808 | tf_op jit(solution)/shard_map/ppermute | solution.py:969
  36.9 27.2 %collective-permute-start.4 = (bf16[2,256,512]{2,1,0:T(8,128)(2,1)S(1)}, bf16[2,256,512]{2,1,0:T(8,128)(2,1)}, u32[]{:S(2)}, u32[]{:S(2)}) collective-permute-start(bf16[2,256,512]{2,1,0:T(8,128)(2,1)S(1)} %pad_maximum_fusion.4.refs_7_.refs_3_), channel_id=1, source_target_pairs={{0,4},{2,6},{4,0},{6,2},{8,12},{10,14},{12,8},{14,10},{16,20},{18,... | collective-permute-start | bytes 1572872 | tf_op jit(solution)/shard_map/ppermute | solution.py:965
  39.0 16.5 %collective-permute-start.1 = (bf16[2,128,512]{2,1,0:T(8,128)(2,1)}, bf16[2,128,512]{2,1,0:T(8,128)(2,1)S(1)}, u32[]{:S(2)}, u32[]{:S(2)}) collective-permute-start(bf16[2,128,512]{2,1,0:T(8,128)(2,1)} %get-tuple-element.221), channel_id=1, source_target_pairs={{0,0},{2,4},{4,8},{6,12},{8,16},{10,20},{12,24},{14,28},{16,30},{1... | collective-permute-start | bytes 786440 | tf_op jit(solution)/shard_map/ppermute | solution.py:1109
  43.7 18.3 %collective-permute-start.2 = (bf16[2,128,512]{2,1,0:T(8,128)(2,1)}, bf16[2,128,512]{2,1,0:T(8,128)(2,1)}, u32[]{:S(2)}, u32[]{:S(2)}) collective-permute-start(bf16[2,128,512]{2,1,0:T(8,128)(2,1)} %get-tuple-element.222), channel_id=1, source_target_pairs={{0,2},{2,6},{4,10},{6,14},{8,18},{10,22},{12,26},{14,30},{16,28},{... | collective-permute-start | bytes 786440 | tf_op jit(solution)/shard_map/ppermute | solution.py:1110
  52.8 29.0 %collective-permute-start.10 = (bf16[2,256,512]{2,1,0:T(8,128)(2,1)S(1)}, bf16[2,256,512]{2,1,0:T(8,128)(2,1)S(1)}, u32[]{:S(2)}, u32[]{:S(2)}) collective-permute-start(bf16[2,256,512]{2,1,0:T(8,128)(2,1)S(1)} %pad_maximum_fusion.5.refs_8_.refs_7_), channel_id=1, source_target_pairs={{0,4},{2,6},{4,0},{6,2},{8,12},{10,14},{12,8},{14,10},{16,20},{18,... | collective-permute-start | bytes 1572872 | tf_op jit(solution)/shard_map/ppermute | solution.py:965
  55.5 40.6 %collective-permute-start.13 = (bf16[1664,512]{1,0:T(8,128)(2,1)}, bf16[1664,512]{1,0:T(8,128)(2,1)}, u32[]{:S(2)}, u32[]{:S(2)}) collective-permute-start(bf16[1664,512]{1,0:T(8,128)(2,1)} %slice_dynamic-update-slice_fusion), channel_id=1, source_target_pairs={{0,1},{1,0},{2,3},{3,2},{4,5},{5,4},{6,7},{7,6},{8,9},{9,8},{10,11... | collective-permute-start | bytes 5111816 | tf_op jit(solution)/shard_map/ppermute | solution.py:969
  122.4 23.7 %collective-permute-start.15 = (bf16[2,2,4,128,512]{4,3,2,1,0:T(8,128)(2,1)}, bf16[2,2,4,128,512]{4,3,2,1,0:T(8,128)(2,1)}, u32[]{:S(2)}, u32[]{:S(2)}) collective-permute-start(bf16[2,2,4,128,512]{4,3,2,1,0:T(8,128)(2,1)} %get-tuple-element.135), channel_id=1, source_target_pairs={{0,2},{2,0},{4,6},{6,4},{8,10},{10,8},{12,14},{14,12},{16,18},{18,... | collective-permute-start | bytes 6291464 | tf_op jit(solution)/shard_map/ppermute | solution.py:965
  137.9 19.7 %collective-permute-start.16 = (bf16[288,512]{1,0:T(8,128)(2,1)}, bf16[288,512]{1,0:T(8,128)(2,1)S(1)}, u32[]{:S(2)}, u32[]{:S(2)}) collective-permute-start(bf16[288,512]{1,0:T(8,128)(2,1)} %get-tuple-element.148.refs_2_), channel_id=1, source_target_pairs={{0,8},{2,10},{4,12},{6,14},{8,0},{10,2},{12,4},{14,6},{16,24},{18,... | collective-permute-start | bytes 884744 | tf_op jit(solution)/shard_map/ppermute | solution.py:965
  155.5 22.1 %collective-permute-start.19 = (bf16[288,512]{1,0:T(8,128)(2,1)S(1)}, bf16[288,512]{1,0:T(8,128)(2,1)S(1)}, u32[]{:S(2)}, u32[]{:S(2)}) collective-permute-start(bf16[288,512]{1,0:T(8,128)(2,1)S(1)} %copy-done.14), channel_id=1, source_target_pairs={{0,24},{2,26},{4,28},{6,30},{8,16},{10,18},{12,20},{14,22},{16,8},... | collective-permute-start | bytes 884744 | tf_op jit(solution)/shard_map/ppermute | solution.py:965
  155.5 25.4 %collective-permute-start.18 = (bf16[288,512]{1,0:T(8,128)(2,1)S(1)}, bf16[288,512]{1,0:T(8,128)(2,1)S(1)}, u32[]{:S(2)}, u32[]{:S(2)}) collective-permute-start(bf16[288,512]{1,0:T(8,128)(2,1)S(1)} %copy-done.14), channel_id=1, source_target_pairs={{0,16},{2,18},{4,20},{6,22},{8,24},{10,26},{12,28},{14,30},{16,0},... | collective-permute-start | bytes 884744 | tf_op jit(solution)/shard_map/ppermute | solution.py:965
  158.5 23.3 %collective-permute-start.20 = (bf16[2,288,512]{2,1,0:T(8,128)(2,1)}, bf16[2,288,512]{2,1,0:T(8,128)(2,1)}, u32[]{:S(2)}, u32[]{:S(2)}) collective-permute-start(bf16[2,288,512]{2,1,0:T(8,128)(2,1)} %pad_maximum_fusion.1.refs_4_), channel_id=1, source_target_pairs={{0,4},{2,6},{4,0},{6,2},{8,12},{10,14},{12,8},{14,10},{16,20},{18,... | collective-permute-start | bytes 1769480 | tf_op jit(solution)/shard_map/ppermute | solution.py:965
  158.5 23.3 %collective-permute-start.17 = (bf16[2,4,128,512]{3,2,1,0:T(8,128)(2,1)S(1)}, bf16[2,4,128,512]{3,2,1,0:T(8,128)(2,1)}, u32[]{:S(2)}, u32[]{:S(2)}) collective-permute-start(bf16[2,4,128,512]{3,2,1,0:T(8,128)(2,1)S(1)} %fusion), channel_id=1, source_target_pairs={{0,1},{1,0},{2,3},{3,2},{4,5},{5,4},{6,7},{7,6},{8,9},{9,8},{10,11... | collective-permute-start | bytes 3145736 | tf_op jit(solution)/shard_map/ppermute | solution.py:969
  194.5 21.7 %collective-permute-start.21 = (bf16[2,2,4,112,512]{4,3,2,1,0:T(8,128)(2,1)}, bf16[2,2,4,112,512]{4,3,2,1,0:T(8,128)(2,1)S(1)}, u32[]{:S(2)}, u32[]{:S(2)}) collective-permute-start(bf16[2,2,4,112,512]{4,3,2,1,0:T(8,128)(2,1)} %get-tuple-element.168), channel_id=1, source_target_pairs={{0,2},{2,0},{4,6},{6,4},{8,10},{10,8},{12,14},{14,12},{16,18},{18,... | collective-permute-start | bytes 5505032 | tf_op jit(solution)/shard_map/ppermute | solution.py:965
  198.4 15.4 %collective-permute-start.25 = (bf16[2,288,512]{2,1,0:T(8,128)(2,1)}, bf16[2,288,512]{2,1,0:T(8,128)(2,1)}, u32[]{:S(2)}, u32[]{:S(2)}) collective-permute-start(bf16[2,288,512]{2,1,0:T(8,128)(2,1)} %pad_maximum_fusion.2.refs_6_), channel_id=1, source_target_pairs={{0,4},{2,6},{4,0},{6,2},{8,12},{10,14},{12,8},{14,10},{16,20},{18,... | collective-permute-start | bytes 1769480 | tf_op jit(solution)/shard_map/ppermute | solution.py:965
  199.9 19.0 %collective-permute-start.22 = (bf16[2,288,512]{2,1,0:T(8,128)(2,1)}, bf16[2,288,512]{2,1,0:T(8,128)(2,1)S(1)}, u32[]{:S(2)}, u32[]{:S(2)}) collective-permute-start(bf16[2,288,512]{2,1,0:T(8,128)(2,1)} %pad_maximum_fusion.1.refs_4_), channel_id=1, source_target_pairs={{0,2},{2,0},{4,6},{6,4},{8,10},{10,8},{12,14},{14,12},{16,18},{18,... | collective-permute-start | bytes 1769480 | tf_op jit(solution)/shard_map/ppermute | solution.py:965
  200.3 20.5 %collective-permute-start.23 = (bf16[2,288,512]{2,1,0:T(8,128)(2,1)}, bf16[2,288,512]{2,1,0:T(8,128)(2,1)}, u32[]{:S(2)}, u32[]{:S(2)}) collective-permute-start(bf16[2,288,512]{2,1,0:T(8,128)(2,1)} %collective-permute-done.20.refs_5_), channel_id=1, source_target_pairs={{0,2},{2,0},{4,6},{6,4},{8,10},{10,8},{12,14},{14,12},{16,18},{18,... | collective-permute-start | bytes 1769480 | tf_op jit(solution)/shard_map/ppermute | solution.py:965
  213.7 19.2 %collective-permute-start.24 = (bf16[4,128,512]{2,1,0:T(8,128)(2,1)S(1)}, bf16[4,128,512]{2,1,0:T(8,128)(2,1)S(1)}, u32[]{:S(2)}, u32[]{:S(2)}) collective-permute-start(bf16[4,128,512]{2,1,0:T(8,128)(2,1)S(1)} %fusion.5), channel_id=1, source_target_pairs={{0,4},{2,6},{4,0},{6,2},{8,12},{10,14},{12,8},{14,10},{16,20},{18,... | collective-permute-start | bytes 1572872 | tf_op jit(solution)/shard_map/ppermute | solution.py:965
  215.1 20.1 %collective-permute-start.26 = (bf16[2,288,512]{2,1,0:T(8,128)(2,1)}, bf16[2,288,512]{2,1,0:T(8,128)(2,1)}, u32[]{:S(2)}, u32[]{:S(2)}) collective-permute-start(bf16[2,288,512]{2,1,0:T(8,128)(2,1)} %pad_maximum_fusion.2.refs_6_), channel_id=1, source_target_pairs={{0,2},{2,0},{4,6},{6,4},{8,10},{10,8},{12,14},{14,12},{16,18},{18,... | collective-permute-start | bytes 1769480 | tf_op jit(solution)/shard_map/ppermute | solution.py:965
  216.3 21.5 %collective-permute-start.27 = (bf16[2,288,512]{2,1,0:T(8,128)(2,1)}, bf16[2,288,512]{2,1,0:T(8,128)(2,1)}, u32[]{:S(2)}, u32[]{:S(2)}) collective-permute-start(bf16[2,288,512]{2,1,0:T(8,128)(2,1)} %collective-permute-done.25.refs_7_), channel_id=1, source_target_pairs={{0,2},{2,0},{4,6},{6,4},{8,10},{10,8},{12,14},{14,12},{16,18},{18,... | collective-permute-start | bytes 1769480 | tf_op jit(solution)/shard_map/ppermute | solution.py:965
  218.9 30.2 %collective-permute-start.31 = (bf16[2,4,112,512]{3,2,1,0:T(8,128)(2,1)S(1)}, bf16[2,4,112,512]{3,2,1,0:T(8,128)(2,1)}, u32[]{:S(2)}, u32[]{:S(2)}) collective-permute-start(bf16[2,4,112,512]{3,2,1,0:T(8,128)(2,1)S(1)} %fusion.2), channel_id=1, source_target_pairs={{0,1},{1,0},{2,3},{3,2},{4,5},{5,4},{6,7},{7,6},{8,9},{9,8},{10,11... | collective-permute-start | bytes 2752520 | tf_op jit(solution)/shard_map/ppermute | solution.py:969
  269.1 25.9 %collective-permute-start.47 = (bf16[4,128,512]{2,1,0:T(8,128)(2,1)S(1)}, bf16[4,128,512]{2,1,0:T(8,128)(2,1)S(1)}, u32[]{:S(2)}, u32[]{:S(2)}) collective-permute-start(bf16[4,128,512]{2,1,0:T(8,128)(2,1)S(1)} %pad_maximum_fusion.6.refs_1_), channel_id=1, source_target_pairs={{0,4},{2,6},{4,0},{6,2},{8,12},{10,14},{12,8},{14,10},{16,20},{18,... | collective-permute-start | bytes 1572872 | tf_op jit(solution)/shard_map/ppermute | solution.py:965
  297.3 16.2 %collective-permute-start.50 = (bf16[144,512]{1,0:T(8,128)(2,1)S(1)}, bf16[144,512]{1,0:T(8,128)(2,1)S(1)}, u32[]{:S(2)}, u32[]{:S(2)}) collective-permute-start(bf16[144,512]{1,0:T(8,128)(2,1)S(1)} %get-tuple-element.227), channel_id=1, source_target_pairs={{0,24},{2,26},{4,28},{6,30},{8,16},{10,18},{12,20},{14,22},{16,8},... | collective-permute-start | bytes 442376 | tf_op jit(solution)/shard_map/ppermute | solution.py:965
  297.8 21.4 %collective-permute-start.52 = (bf16[4,128,512]{2,1,0:T(8,128)(2,1)S(1)}, bf16[4,128,512]{2,1,0:T(8,128)(2,1)S(1)}, u32[]{:S(2)}, u32[]{:S(2)}) collective-permute-start(bf16[4,128,512]{2,1,0:T(8,128)(2,1)S(1)} %pad_maximum_fusion.6.refs_1_), channel_id=1, source_target_pairs={{0,2},{2,0},{4,6},{6,4},{8,10},{10,8},{12,14},{14,12},{16,18},{18,... | collective-permute-start | bytes 1572872 | tf_op jit(solution)/shard_map/ppermute | solution.py:965
  299.9 19.3 %collective-permute-start.53 = (bf16[4,128,512]{2,1,0:T(8,128)(2,1)S(1)}, bf16[4,128,512]{2,1,0:T(8,128)(2,1)S(1)}, u32[]{:S(2)}, u32[]{:S(2)}) collective-permute-start(bf16[4,128,512]{2,1,0:T(8,128)(2,1)S(1)} %collective-permute-done.47.refs_2_), channel_id=1, source_target_pairs={{0,2},{2,0},{4,6},{6,4},{8,10},{10,8},{12,14},{14,12},{16,18},{18,... | collective-permute-start | bytes 1572872 | tf_op jit(solution)/shard_map/ppermute | solution.py:965
  313.6 19.5 %collective-permute-start.51 = (bf16[4,144,512]{2,1,0:T(8,128)(2,1)S(1)}, bf16[4,144,512]{2,1,0:T(8,128)(2,1)S(1)}, u32[]{:S(2)}, u32[]{:S(2)}) collective-permute-start(bf16[4,144,512]{2,1,0:T(8,128)(2,1)S(1)} %pad_maximum_fusion.3.own_ref), channel_id=1, source_target_pairs={{0,4},{2,6},{4,0},{6,2},{8,12},{10,14},{12,8},{14,10},{16,20},{18,... | collective-permute-start | bytes 1769480 | tf_op jit(solution)/shard_map/ppermute | solution.py:965
  314.6 22.0 %collective-permute-start.32 = (bf16[2,128,512]{2,1,0:T(8,128)(2,1)S(1)}, bf16[2,128,512]{2,1,0:T(8,128)(2,1)S(1)}, u32[]{:S(2)}, u32[]{:S(2)}) collective-permute-start(bf16[2,128,512]{2,1,0:T(8,128)(2,1)S(1)} %get-tuple-element.214), channel_id=1, source_target_pairs={{0,0},{4,2},{8,4},{12,6},{16,8},{20,10},{24,12},{28,14},{30,16},{2... | collective-permute-start | bytes 786440 | tf_op jit(solution)/shard_map/ppermute | solution.py:1336
  316.5 20.1 %collective-permute-start.33 = (bf16[2,128,512]{2,1,0:T(8,128)(2,1)S(1)}, bf16[2,128,512]{2,1,0:T(8,128)(2,1)S(1)}, u32[]{:S(2)}, u32[]{:S(2)}) collective-permute-start(bf16[2,128,512]{2,1,0:T(8,128)(2,1)S(1)} %get-tuple-element.215), channel_id=1, source_target_pairs={{2,0},{6,2},{10,4},{14,6},{18,8},{22,10},{26,12},{30,14},{28,16},{... | collective-permute-start | bytes 786440 | tf_op jit(solution)/shard_map/ppermute | solution.py:1336
  (66 other events, 556.1 us)
Sparse Core Ops, SparseCore 0:
  10.9 53.2 all-gather.2
  259.3 64.4 reduce-scatter.1

commit v2 on v1

--- a/solution.py
+++ b/solution.py
@@ -338,17 +338,23 @@
         base = pl.multiple_of(index * key_rows, key_rows)
         key_pos = base + lax.broadcasted_iota(jnp.int32, (key_rows, 1), 0)
         allowed = (key_pos >= low2) & (key_pos <= high2)
+        def tile_at(pair, offset):
+            start = offset + pair * tile_width
+            return pl.ds(base, key_rows), slice(start, start + tile_width)
+
+        def products(pair):
+            return (
+                dot_nt(kv_ref[tile_at(pair, 0)], q2[pair]),
+                dot_nt(kv_ref[tile_at(pair, width)], g2[pair]),
+            )
+
+        ahead = products(0)
         for pair in range(PAIRS):
-            key_at = (pl.ds(base, key_rows), slice(pair * tile_width, (pair + 1) * tile_width))
-            value_at = (
-                pl.ds(base, key_rows),
-                slice(width + pair * tile_width, width + (pair + 1) * tile_width),
-            )
-            keys = kv_ref[key_at]
-            values = kv_ref[value_at]
-            scores = dot_nt(keys, q2[pair])
+            key_at, value_at = tile_at(pair, 0), tile_at(pair, width)
+            scores, prob_grad = ahead
+            if pair + 1 < PAIRS:
+                ahead = products(pair + 1)
             probs = jnp.where(allowed, jnp.exp2(scores * factor - log_rows[pair]), 0.0)
-            prob_grad = dot_nt(values, g2[pair])
             score_grad = (probs * (prob_grad - delta_rows[pair])).astype(bf16)
             key_grad = dot_nn(score_grad, q2[pair]) * scale
             value_grad = dot_nn(probs.astype(bf16), g2[pair])
@@ -357,7 +363,7 @@
                 value_grad = value_grad + dkv_ref[value_at].astype(f32)
             dkv_ref[key_at] = key_grad.astype(bf16)
             dkv_ref[value_at] = value_grad.astype(bf16)
-            dq_ref[pair] += dot_tn(keys, score_grad)
+            dq_ref[pair] += dot_tn(kv_ref[key_at], score_grad)
         return carry
 
     lax.fori_loop(first, last, step, 0)
@@ -628,7 +634,7 @@
     h2_ref[...] = h2_low
     u = dot_nn(h2_low, u_ref[...]) + ffn_bias_ref[...]
     sig = 1.0 / (1.0 + jnp.exp(-u))
-    act = (u / (1.0 + jnp.exp(-u))).astype(bf16)
+    act = (u * sig).astype(bf16)
     f_ref[...] = act
     slope = sig * (1.0 + u * (1.0 - sig))
     r3 = h2 + (dot_nn(act, v_ref[...]) + bias_ref[8:9, :])
@@ -936,7 +942,8 @@
     lanes = gain_ref.shape[1]
     gain_ref[...] = rest_ref[0:3, 0:lanes]
     bias_ref[...] = rest_ref[3:13, 0:lanes]
-    shift_ref[...] = rest_ref[16:20, 0:lanes]
+    for k in range(4):
+        shift_ref[:, k * lanes : (k + 1) * lanes] = rest_ref[16 + k : 17 + k, 0:lanes]
 
 
 def call_kernel(kernel, inputs, outputs, scratch, name, micros, in_place=()):
@@ -1380,7 +1387,7 @@
             (info, *spread_chips(spread_planes(maps), up)),
             (
                 (in_proj.shape, f32), (out_proj.shape, f32), ((3, lanes), f32), ((10, lanes), f32),
-                ((4, lanes), f32),
+                ((1, 4 * lanes), f32),
             ),
             [((half_rows, width), f32)],
             "place_maps",

time: 357 us -> 351 us (0.983)
    unnamed x89 -> x88, local copies, waits for them, and re-layouts: 17.5 us -> 16.3 us
  transfers between devices with their start and end apart: 58 -> 58, of which waited for: 20 -> 20; matrix products, arithmetic and copies ran while one was open for 13% -> 14% of each run, Pallas kernels for 26% -> 25%
where the time goes in v2:
time: 351 us; the launch traced here: 347 us
  Pallas kernels  127 us (36%)
  starting transfers between devices  72.2 us (21%)
  waiting for transfers between devices  71.5 us (20%)
  other arithmetic  33.5 us (10%)
  local copies, waits for them, and re-layouts  28 us (8%)
  between operations  15.2 us (4%)
    pallas_call x13, Pallas kernels, call_kernel(): pl.pallas_call(kernel, in_specs=[smem] + [pl.BlockSpec(memory_space=pl.AN...  127 us
    ppermute x47, waiting for transfers between devices, exchange(): return lax.ppermute(value, 'ctx', [(i, i ^ bits) for i in range(count)])  65.1 us
    ppermute x47, starting transfers between devices, exchange(): return lax.ppermute(value, 'ctx', [(i, i ^ bits) for i in range(count)])  55.6 us
    unnamed x88, local copies, waits for them, and re-layouts  16.3 us
  transfers between devices with their start and end apart: 58, of which 20 were waited for; matrix products, arithmetic and copies ran while one was open for 14% of the time, Pallas kernels for 25%

profile of v2, /device:TPU:9, one launch (start us, length us, event | category | flops | bytes accessed | tf_op | source)
XLA Modules:
  0.0 347.4 jit_solution(7801399838112700050)
XLA Ops:
  13.0 3.0 fusion.37
  39.0 4.7 %collective-permute-start.1 = (bf16[2,128,512]{2,1,0:T(8,128)(2,1)}, bf16[2,128,512]{2,1,0:T(8,128)(2,1)S(1)}, u32[]{:S(2)}, u32[]{:S(2)}) collective-permute-start(bf16[2,128,512]{2,1,0:T(8,128)(2,1)} %get-tuple-element.221), channel_id=1, source_target_pairs={{0,0},{2,4},{4,8},{6,12},{8,16},{10,20},{12,24},{14,28},{16,30},{1... | collective-permute-start | bytes 786440 | tf_op jit(solution)/shard_map/ppermute | solution.py:1116
  52.8 2.7 collective-permute-start.10
  55.7 6.4 %collective-permute-done.2 = bf16[2,128,512]{2,1,0:T(8,128)(2,1)} collective-permute-done((bf16[2,128,512]{2,1,0:T(8,128)(2,1)}, bf16[2,128,512]{2,1,0:T(8,128)(2,1)}, u32[]{:S(2)}, u32[]{:S(2)}) %collective-permute-start.2) | collective-permute-done | bytes 262176 | tf_op jit(solution)/shard_map/ppermute | solution.py:1117
  68.5 13.3 %first_forward.1 = (bf16[256,512]{1,0:T(8,128)(2,1)}, bf16[256,1024]{1,0:T(8,128)(2,1)}, bf16[2048,1024]{1,0:T(8,128)(2,1)}, bf16[3,512,512]{2,1,0:T(8,128)(2,1)...) custom-call(s32[8,256]{1,0:T(8,128)} %copy-done.18, bf16[256,512]{1,0:T(8,128)(2,1)} %get-tuple-element.220.refs_1_.refs_18_, ...), custom_call_target="tpu_custom_call" | custom-call | flops 10000000000 | bytes 100000 | tf_op jit(solution)/shard_map/first_forward/pallas_call | solution.py:952
  85.3 10.8 %second_forward.1 = (f32[256,512]{1,0:T(8,128)}, f32[8,256]{1,0:T(8,128)}, bf16[2048,1024]{1,0:T(8,128)(2,1)}) custom-call(s32[8,256]{1,0:T(8,128)} %copy-done.18, bf16[2048,1024]{1,0:T(8,128)(2,1)} %get-tuple-element.112.refs_1_.refs_3_, bf16[256,512]{1,0:T(8,128)(2,1)} %get-tuple-element.150.refs_2_.refs_1_, f32[10,512]{1,0:T(8,128)} %bitcast.153, ...), custom_call_target="tpu_custom_call" | custom-call | flops 10000000000 | bytes 100000 | tf_op jit(solution)/shard_map/second_forward/pallas_call | solution.py:952
  101.2 15.9 %middle_forward.1 = (f32[256,512]{1,0:T(8,128)}, bf16[256,512]{1,0:T(8,128)(2,1)}, bf16[256,512]{1,0:T(8,128)(2,1)}, bf16[256,512]{1,0:T(8,128)(2,1)}, bf16[256,...) custom-call(s32[8,256]{1,0:T(8,128)} %copy-done.18, ...), custom_call_target="tpu_custom_call" | custom-call | flops 24999999488 | bytes 250000 | tf_op jit(solution)/shard_map/middle_forward/pallas_call | solution.py:952
  117.1 5.3 %feed_grads.1 = (bf16[2,2,4,128,512]{4,3,2,1,0:T(8,128)(2,1)}, bf16[2,2,4,128,512]{4,3,2,1,0:T(8,128)(2,1)}) custom-call(s32[8,256]{1,0:T(8,128)} %copy-done.18, bf16[256,512]{1,0:T(8,128)(2,1)} %get-tuple-element.130.refs_1_, bf16[256,2048]{1,0:T(8,128)(2,1)} %get-tuple-element.131.refs_2_, bf16[256,2048]{1,0:T(8,128)(2,1)} %get-tuple-element.132.refs_3_, ...), custom_call_target="tpu_custom_call" | custom-call | flops 5000000000 | bytes 50000 | tf_op jit(solution)/shard_map/feed_grads/pallas_call | solution.py:952
  122.8 13.3 %middle_backward.1 = (bf16[256,512]{1,0:T(8,128)(2,1)}, bf16[256,512]{1,0:T(8,128)(2,1)}, bf16[288,512]{1,0:T(8,128)(2,1)}, f32[256,512]{1,0:T(8,128)}, f32[8,25...) custom-call(s32[8,256]{1,0:T(8,128)} %copy-done.18, f32[256,512]{1,0:T(8,128)} %get-tuple-element.119.refs_2_.refs_1_, ...), custom_call_target="tpu_custom_call" | custom-call | flops 14000000000 | bytes 140000 | tf_op jit(solution)/shard_map/middle_backward/pallas_call | solution.py:952
  136.1 8.1 %collective-permute-start.16 = (bf16[288,512]{1,0:T(8,128)(2,1)}, bf16[288,512]{1,0:T(8,128)(2,1)S(1)}, u32[]{:S(2)}, u32[]{:S(2)}) collective-permute-start(bf16[288,512]{1,0:T(8,128)(2,1)} %get-tuple-element.148.refs_2_), channel_id=1, source_target_pairs={{0,8},{2,10},{4,12},{6,14},{8,0},{10,2},{12,4},{14,6},{16,24},{18,... | collective-permute-start | bytes 884744 | tf_op jit(solution)/shard_map/ppermute | solution.py:972
  145.7 7.8 %memory_grads.1 = (bf16[2048,512]{1,0:T(8,128)(2,1)}, bf16[512,1024]{1,0:T(8,128)(2,1)}) custom-call(s32[8,256]{1,0:T(8,128)} %copy-done.18, bf16[2048,512]{1,0:T(8,128)(2,1)} %bitcast.166, bf16[5,512,512]{2,1,0:T(8,128)(2,1)} %get-tuple-element.127.refs_5_.refs_2_, bf16[2048,1024]{1,0:T(8,128)(2,1)} %get-tuple-element.146.refs_3_), custom_call_target="tpu_custom_call" | custom-call | flops 5000000000 | bytes 50000 | tf_op jit(solution)/shard_map/memory_grads/pallas_call | solution.py:952
  153.5 2.8 collective-permute-start.18
  158.8 16.1 %query_backward.1.refs_19_.refs_3_ = bf16[256,512]{1,0:T(8,128)(2,1)} custom-call(s32[8,256]{1,0:T(8,128)} %copy-done.18, bf16[256,512]{1,0:T(8,128)(2,1)} %get-tuple-element.150.refs_2_.refs_1_, bf16[288,512]{1,0:T(8,128)(2,1)} %get-tuple-element.148.refs_2_, bf16[2048,1024]{1,0:T(8,128)(2,1)} %get-tuple-element.112.refs_1_.refs_3_, ...), custom_call_target="tpu_custom_call" | custom-call | flops 20000000000 | bytes 200000 | tf_op jit(solution)/shard_map/query_backward/pallas_call | solution.py:952
  174.9 3.7 %collective-permute-done.18 = bf16[288,512]{1,0:T(8,128)(2,1)S(1)} collective-permute-done((bf16[288,512]{1,0:T(8,128)(2,1)S(1)}, bf16[288,512]{1,0:T(8,128)(2,1)S(1)}, u32[]{:S(2)}, u32[]{:S(2)}) %collective-permute-start.18) | collective-permute-done | bytes 294944 | tf_op jit(solution)/shard_map/ppermute | solution.py:972
  181.9 10.3 %grads_project.1 = (bf16[4096,512]{1,0:T(8,128)(2,1)}, bf16[2,2,4,112,512]{4,3,2,1,0:T(8,128)(2,1)}, bf16[2,2,4,112,512]{4,3,2,1,0:T(8,128)(2,1)}) custom-call(s32[8,256]{1,0:T(8,128)} %copy-done.18, bf16[3,512,512]{2,1,0:T(8,128)(2,1)} %get-tuple-element.114.refs_5_.refs_1_.refs_6_, f32[10,512]{1,0:T(8,128)} %bitcast.155, bf16[2,256,512]{2,1,0:T(8,128)(2,1)} %copy-done.10, ...), custom_call_target="tpu_custom_call" | custom-call | flops 12000000000 | bytes 120000 | tf_op jit(solution)/shard_map/grads_project/pallas_call | solution.py:952
  192.2 3.5 %collective-permute-start.21 = (bf16[2,2,4,112,512]{4,3,2,1,0:T(8,128)(2,1)}, bf16[2,2,4,112,512]{4,3,2,1,0:T(8,128)(2,1)S(1)}, u32[]{:S(2)}, u32[]{:S(2)}) collective-permute-start(bf16[2,2,4,112,512]{4,3,2,1,0:T(8,128)(2,1)} %get-tuple-element.168), channel_id=1, source_target_pairs={{0,2},{2,0},{4,6},{6,4},{8,10},{10,8},{12,14},{14,12},{16,18},{18,... | collective-permute-start | bytes 5505032 | tf_op jit(solution)/shard_map/ppermute | solution.py:972
  197.7 13.2 %collective-permute-done.25.refs_7_ = bf16[2,288,512]{2,1,0:T(8,128)(2,1)} collective-permute-done((bf16[2,288,512]{2,1,0:T(8,128)(2,1)}, bf16[2,288,512]{2,1,0:T(8,128)(2,1)}, u32[]{:S(2)}, u32[]{:S(2)}) %collective-permute-start.25) | collective-permute-done | bytes 589856 | tf_op jit(solution)/shard_map/ppermute | solution.py:972
  217.7 12.2 %key_backward.1 = (f32[2,4,256,128]{3,2,1,0:T(8,128)}, f32[2,4,256,128]{3,2,1,0:T(8,128)}) custom-call(s32[8,256]{1,0:T(8,128)} %copy-done.18, bf16[256,1024]{1,0:T(8,128)(2,1)} %get-tuple-element.171.refs_1_, bf16[4096,512]{1,0:T(8,128)(2,1)} %get-tuple-element.169.refs_2_, s32[256,8]{1,0:T(8,128)} %copy.30.refs_3_.refs_4_.refs_7_, ...), custom_call_target="tpu_custom_call" | custom-call | flops 8000000000 | bytes 80000 | tf_op jit(solution)/shard_map/key_backward/pallas_call | solution.py:952
  234.7 10.7 %key_backward_last.1 = (bf16[256,512]{1,0:T(8,128)(2,1)}, bf16[256,512]{1,0:T(8,128)(2,1)}) custom-call(s32[8,256]{1,0:T(8,128)} %copy-done.18, bf16[256,1024]{1,0:T(8,128)(2,1)} %get-tuple-element.171.refs_1_, bf16[4096,512]{1,0:T(8,128)(2,1)} %get-tuple-element.169.refs_2_, s32[256,8]{1,0:T(8,128)} %copy.30.refs_3_.refs_4_.refs_7_, ...), custom_call_target="tpu_custom_call" | custom-call | flops 3000000000 | bytes 30000 | tf_op jit(solution)/shard_map/key_backward_last/pallas_call | solution.py:952
  248.3 3.8 %self_grads.1 = (bf16[256,512]{1,0:T(8,128)(2,1)}, bf16[2,2,4,32,512]{4,3,2,1,0:T(8,128)(2,1)}, bf16[2,2,4,32,512]{4,3,2,1,0:T(8,128)(2,1)}) custom-call(s32[8,256]{1,0:T(8,128)} %copy-done.18, bf16[256,512]{1,0:T(8,128)(2,1)} %get-tuple-element.220.refs_1_.refs_18_, f32[256,512]{1,0:T(8,128)} %get-tuple-element.143.refs_2_, ...), custom_call_target="tpu_custom_call" | custom-call | flops 4000000000 | bytes 40000 | tf_op jit(solution)/shard_map/self_grads/pallas_call | solution.py:952
  253.2 2.8 collective-permute-start.41
  256.4 7.8 %collective-permute-done.42 = bf16[128,512]{1,0:T(8,128)(2,1)S(1)} collective-permute-done((bf16[128,512]{1,0:T(8,128)(2,1)}, bf16[128,512]{1,0:T(8,128)(2,1)S(1)}, u32[]{:S(2)}, u32[]{:S(2)}) %collective-permute-start.42) | collective-permute-done | bytes 131104 | tf_op jit(solution)/shard_map/ppermute | solution.py:972
  268.6 2.7 collective-permute-start.35
  275.9 4.8 %collective-permute-done.36 = bf16[112,512]{1,0:T(8,128)(2,1)S(1)} collective-permute-done((bf16[112,512]{1,0:T(8,128)(2,1)S(1)}, bf16[112,512]{1,0:T(8,128)(2,1)S(1)}, u32[]{:S(2)}, u32[]{:S(2)}) %collective-permute-start.36) | collective-permute-done | bytes 114720 | tf_op jit(solution)/shard_map/ppermute | solution.py:972
  281.6 3.3 collective-permute-start.45
  287.7 4.3 %collective-permute-done.46 = bf16[32,512]{1,0:T(8,128)(2,1)S(1)} collective-permute-done((bf16[32,512]{1,0:T(8,128)(2,1)S(1)}, bf16[32,512]{1,0:T(8,128)(2,1)S(1)}, u32[]{:S(2)}, u32[]{:S(2)}) %collective-permute-start.46) | collective-permute-done | bytes 32800 | tf_op jit(solution)/shard_map/ppermute | solution.py:972
  297.0 5.0 %collective-permute-done.49 = bf16[144,512]{1,0:T(8,128)(2,1)S(1)} collective-permute-done((bf16[144,512]{1,0:T(8,128)(2,1)S(1)}, bf16[144,512]{1,0:T(8,128)(2,1)S(1)}, u32[]{:S(2)}, u32[]{:S(2)}) %collective-permute-start.49) | collective-permute-done | bytes 147488 | tf_op jit(solution)/shard_map/ppermute | solution.py:972
  303.7 6.8 %collective-permute-done.50 = bf16[144,512]{1,0:T(8,128)(2,1)S(1)} collective-permute-done((bf16[144,512]{1,0:T(8,128)(2,1)S(1)}, bf16[144,512]{1,0:T(8,128)(2,1)S(1)}, u32[]{:S(2)}, u32[]{:S(2)}) %collective-permute-start.50) | collective-permute-done | bytes 147488 | tf_op jit(solution)/shard_map/ppermute | solution.py:972
  313.5 2.6 collective-permute-start.33
  317.8 3.9 %place_feed.1 = (f32[256,2048]{1,0:T(8,128)}, f32[1024,512]{1,0:T(8,128)}) custom-call(s32[8,256]{1,0:T(8,128)} %copy-done.18, bf16[4,128,512]{2,1,0:T(8,128)(2,1)} %copy-done.12, bf16[4,128,512]{2,1,0:T(8,128)(2,1)} %copy-done.34, bf16[4,128,512]{2,1,0:T(8,128)(2,1)} %copy-done.37, bf16[4,128,512]{2,1,0:T(8,128)(2,1)} %copy-done.38), custom_call_target="tpu_custom_call" | custom-call | flops 4000000000 | bytes 40000 | tf_op jit(solution)/shard_map/place_feed/pallas_call | solution.py:952
  322.1 7.7 %collective-permute-done.51.other_ref = bf16[4,144,512]{2,1,0:T(8,128)(2,1)S(1)} collective-permute-done((bf16[4,144,512]{2,1,0:T(8,128)(2,1)S(1)}, bf16[4,144,512]{2,1,0:T(8,128)(2,1)S(1)}, u32[]{:S(2)}, u32[]{:S(2)}) %collective-permute-start.51) | collective-permute-done | bytes 589856 | tf_op jit(solution)/shard_map/ppermute | solution.py:972
  336.4 3.7 %place_maps.1 = (f32[6,256,512]{2,1,0:T(8,128)}, f32[2,256,512]{2,1,0:T(8,128)}, f32[3,256]{1,0:T(4,128)}, f32[10,256]{1,0:T(8,128)}, f32[1,1024]{1,0:T(1,128)}) custom-call(s32[8,256]{1,0:T(8,128)} %copy-done.18, bf16[4,144,512]{2,1,0:T(8,128)(2,1)} %copy-done.7, bf16[4,144,512]{2,1,0:T(8,128)(2,1)} %copy-done.27, bf16[4,144,512]{2,1,0:T(8,128)(2,1)} %copy-done.28, ...), custom_call_target="tpu_custom_call" | custom-call | flops 4000000000 | bytes 40000 | tf_op jit(solution)/shard_map/place_maps/pallas_call | solution.py:952
  (265 shorter events, 109.2 us)
Async XLA Ops:
  7.2 92.8 %all-gather.3.cloned.1.call-start = ((), (), s32[]{:S(2)}) async-start(), calls=%async_computation.2 | async-start | bytes 2228224 | tf_op jit(solution)/shard_map/all_gather | solution.py:1127
  7.2 36.5 %collective-permute-start.7 = (bf16[256,512]{1,0:T(8,128)(2,1)}, bf16[256,512]{1,0:T(8,128)(2,1)S(1)}, u32[]{:S(2)}, u32[]{:S(2)}) collective-permute-start(bf16[256,512]{1,0:T(8,128)(2,1)} %bitcast.137), channel_id=1, source_target_pairs={{0,24},{2,26},{4,28},{6,30},{8,16},{10,18},{12,20},{14,22},{16,8},... | collective-permute-start | bytes 786440 | tf_op jit(solution)/shard_map/ppermute | solution.py:972
  8.6 43.2 %collective-permute-start.6 = (bf16[256,512]{1,0:T(8,128)(2,1)}, bf16[256,512]{1,0:T(8,128)(2,1)}, u32[]{:S(2)}, u32[]{:S(2)}) collective-permute-start(bf16[256,512]{1,0:T(8,128)(2,1)} %bitcast.138), channel_id=1, source_target_pairs={{0,16},{2,18},{4,20},{6,22},{8,24},{10,26},{12,28},{14,30},{16,0},... | collective-permute-start | bytes 786440 | tf_op jit(solution)/shard_map/ppermute | solution.py:972
  9.7 25.5 %collective-permute-start = (bf16[256,512]{1,0:T(8,128)(2,1)}, bf16[256,512]{1,0:T(8,128)(2,1)}, u32[]{:S(2)}, u32[]{:S(2)}) collective-permute-start(bf16[256,512]{1,0:T(8,128)(2,1)} %bitcast.139), channel_id=1, source_target_pairs={{0,8},{2,10},{4,12},{6,14},{8,0},{10,2},{12,4},{14,6},{16,24},{18,... | collective-permute-start | bytes 786440 | tf_op jit(solution)/shard_map/ppermute | solution.py:972
  10.8 321.2 %reduce-scatter.2.cloned.1.call-start = ((), (), s32[]{:S(2)}) async-start(), calls=%async_computation.1 | async-start | bytes 2228224 | tf_op jit(solution)/shard_map/reduce_scatter | solution.py:1290
  18.0 33.4 %collective-permute-start.3 = (bf16[400,512]{1,0:T(8,128)(2,1)}, bf16[400,512]{1,0:T(8,128)(2,1)}, u32[]{:S(2)}, u32[]{:S(2)}) collective-permute-start(bf16[400,512]{1,0:T(8,128)(2,1)} %pad_maximum_fusion.7), channel_id=1, source_target_pairs={{0,1},{1,0},{2,3},{3,2},{4,5},{5,4},{6,7},{7,6},{8,9},{9,8},{10,11... | collective-permute-start | bytes 1228808 | tf_op jit(solution)/shard_map/ppermute | solution.py:976
  36.9 27.2 %collective-permute-start.4 = (bf16[2,256,512]{2,1,0:T(8,128)(2,1)S(1)}, bf16[2,256,512]{2,1,0:T(8,128)(2,1)}, u32[]{:S(2)}, u32[]{:S(2)}) collective-permute-start(bf16[2,256,512]{2,1,0:T(8,128)(2,1)S(1)} %pad_maximum_fusion.4.refs_7_.refs_3_), channel_id=1, source_target_pairs={{0,4},{2,6},{4,0},{6,2},{8,12},{10,14},{12,8},{14,10},{16,20},{18,... | collective-permute-start | bytes 1572872 | tf_op jit(solution)/shard_map/ppermute | solution.py:972
  39.0 16.5 %collective-permute-start.1 = (bf16[2,128,512]{2,1,0:T(8,128)(2,1)}, bf16[2,128,512]{2,1,0:T(8,128)(2,1)S(1)}, u32[]{:S(2)}, u32[]{:S(2)}) collective-permute-start(bf16[2,128,512]{2,1,0:T(8,128)(2,1)} %get-tuple-element.221), channel_id=1, source_target_pairs={{0,0},{2,4},{4,8},{6,12},{8,16},{10,20},{12,24},{14,28},{16,30},{1... | collective-permute-start | bytes 786440 | tf_op jit(solution)/shard_map/ppermute | solution.py:1116
  43.7 18.3 %collective-permute-start.2 = (bf16[2,128,512]{2,1,0:T(8,128)(2,1)}, bf16[2,128,512]{2,1,0:T(8,128)(2,1)}, u32[]{:S(2)}, u32[]{:S(2)}) collective-permute-start(bf16[2,128,512]{2,1,0:T(8,128)(2,1)} %get-tuple-element.222), channel_id=1, source_target_pairs={{0,2},{2,6},{4,10},{6,14},{8,18},{10,22},{12,26},{14,30},{16,28},{... | collective-permute-start | bytes 786440 | tf_op jit(solution)/shard_map/ppermute | solution.py:1117
  52.8 29.0 %collective-permute-start.10 = (bf16[2,256,512]{2,1,0:T(8,128)(2,1)S(1)}, bf16[2,256,512]{2,1,0:T(8,128)(2,1)S(1)}, u32[]{:S(2)}, u32[]{:S(2)}) collective-permute-start(bf16[2,256,512]{2,1,0:T(8,128)(2,1)S(1)} %pad_maximum_fusion.5.refs_8_.refs_7_), channel_id=1, source_target_pairs={{0,4},{2,6},{4,0},{6,2},{8,12},{10,14},{12,8},{14,10},{16,20},{18,... | collective-permute-start | bytes 1572872 | tf_op jit(solution)/shard_map/ppermute | solution.py:972
  55.5 40.6 %collective-permute-start.13 = (bf16[1664,512]{1,0:T(8,128)(2,1)}, bf16[1664,512]{1,0:T(8,128)(2,1)}, u32[]{:S(2)}, u32[]{:S(2)}) collective-permute-start(bf16[1664,512]{1,0:T(8,128)(2,1)} %slice_dynamic-update-slice_fusion), channel_id=1, source_target_pairs={{0,1},{1,0},{2,3},{3,2},{4,5},{5,4},{6,7},{7,6},{8,9},{9,8},{10,11... | collective-permute-start | bytes 5111816 | tf_op jit(solution)/shard_map/ppermute | solution.py:976
  122.4 21.7 %collective-permute-start.15 = (bf16[2,2,4,128,512]{4,3,2,1,0:T(8,128)(2,1)}, bf16[2,2,4,128,512]{4,3,2,1,0:T(8,128)(2,1)}, u32[]{:S(2)}, u32[]{:S(2)}) collective-permute-start(bf16[2,2,4,128,512]{4,3,2,1,0:T(8,128)(2,1)} %get-tuple-element.135), channel_id=1, source_target_pairs={{0,2},{2,0},{4,6},{6,4},{8,10},{10,8},{12,14},{14,12},{16,18},{18,... | collective-permute-start | bytes 6291464 | tf_op jit(solution)/shard_map/ppermute | solution.py:972
  136.1 20.3 %collective-permute-start.16 = (bf16[288,512]{1,0:T(8,128)(2,1)}, bf16[288,512]{1,0:T(8,128)(2,1)S(1)}, u32[]{:S(2)}, u32[]{:S(2)}) collective-permute-start(bf16[288,512]{1,0:T(8,128)(2,1)} %get-tuple-element.148.refs_2_), channel_id=1, source_target_pairs={{0,8},{2,10},{4,12},{6,14},{8,0},{10,2},{12,4},{14,6},{16,24},{18,... | collective-permute-start | bytes 884744 | tf_op jit(solution)/shard_map/ppermute | solution.py:972
  153.5 21.4 %collective-permute-start.19 = (bf16[288,512]{1,0:T(8,128)(2,1)S(1)}, bf16[288,512]{1,0:T(8,128)(2,1)S(1)}, u32[]{:S(2)}, u32[]{:S(2)}) collective-permute-start(bf16[288,512]{1,0:T(8,128)(2,1)S(1)} %copy-done.14), channel_id=1, source_target_pairs={{0,24},{2,26},{4,28},{6,30},{8,16},{10,18},{12,20},{14,22},{16,8},... | collective-permute-start | bytes 884744 | tf_op jit(solution)/shard_map/ppermute | solution.py:972
  153.5 25.1 %collective-permute-start.18 = (bf16[288,512]{1,0:T(8,128)(2,1)S(1)}, bf16[288,512]{1,0:T(8,128)(2,1)S(1)}, u32[]{:S(2)}, u32[]{:S(2)}) collective-permute-start(bf16[288,512]{1,0:T(8,128)(2,1)S(1)} %copy-done.14), channel_id=1, source_target_pairs={{0,16},{2,18},{4,20},{6,22},{8,24},{10,26},{12,28},{14,30},{16,0},... | collective-permute-start | bytes 884744 | tf_op jit(solution)/shard_map/ppermute | solution.py:972
  157.3 22.3 %collective-permute-start.20 = (bf16[2,288,512]{2,1,0:T(8,128)(2,1)}, bf16[2,288,512]{2,1,0:T(8,128)(2,1)}, u32[]{:S(2)}, u32[]{:S(2)}) collective-permute-start(bf16[2,288,512]{2,1,0:T(8,128)(2,1)} %pad_maximum_fusion.1.refs_4_), channel_id=1, source_target_pairs={{0,4},{2,6},{4,0},{6,2},{8,12},{10,14},{12,8},{14,10},{16,20},{18,... | collective-permute-start | bytes 1769480 | tf_op jit(solution)/shard_map/ppermute | solution.py:972
  157.3 22.3 %collective-permute-start.17 = (bf16[2,4,128,512]{3,2,1,0:T(8,128)(2,1)S(1)}, bf16[2,4,128,512]{3,2,1,0:T(8,128)(2,1)}, u32[]{:S(2)}, u32[]{:S(2)}) collective-permute-start(bf16[2,4,128,512]{3,2,1,0:T(8,128)(2,1)S(1)} %fusion), channel_id=1, source_target_pairs={{0,1},{1,0},{2,3},{3,2},{4,5},{5,4},{6,7},{7,6},{8,9},{9,8},{10,11... | collective-permute-start | bytes 3145736 | tf_op jit(solution)/shard_map/ppermute | solution.py:976
  192.2 21.3 %collective-permute-start.21 = (bf16[2,2,4,112,512]{4,3,2,1,0:T(8,128)(2,1)}, bf16[2,2,4,112,512]{4,3,2,1,0:T(8,128)(2,1)S(1)}, u32[]{:S(2)}, u32[]{:S(2)}) collective-permute-start(bf16[2,2,4,112,512]{4,3,2,1,0:T(8,128)(2,1)} %get-tuple-element.168), channel_id=1, source_target_pairs={{0,2},{2,0},{4,6},{6,4},{8,10},{10,8},{12,14},{14,12},{16,18},{18,... | collective-permute-start | bytes 5505032 | tf_op jit(solution)/shard_map/ppermute | solution.py:972
  195.7 15.2 %collective-permute-start.25 = (bf16[2,288,512]{2,1,0:T(8,128)(2,1)}, bf16[2,288,512]{2,1,0:T(8,128)(2,1)}, u32[]{:S(2)}, u32[]{:S(2)}) collective-permute-start(bf16[2,288,512]{2,1,0:T(8,128)(2,1)} %pad_maximum_fusion.2.refs_6_), channel_id=1, source_target_pairs={{0,4},{2,6},{4,0},{6,2},{8,12},{10,14},{12,8},{14,10},{16,20},{18,... | collective-permute-start | bytes 1769480 | tf_op jit(solution)/shard_map/ppermute | solution.py:972
  197.2 19.0 %collective-permute-start.22 = (bf16[2,288,512]{2,1,0:T(8,128)(2,1)}, bf16[2,288,512]{2,1,0:T(8,128)(2,1)S(1)}, u32[]{:S(2)}, u32[]{:S(2)}) collective-permute-start(bf16[2,288,512]{2,1,0:T(8,128)(2,1)} %pad_maximum_fusion.1.refs_4_), channel_id=1, source_target_pairs={{0,2},{2,0},{4,6},{6,4},{8,10},{10,8},{12,14},{14,12},{16,18},{18,... | collective-permute-start | bytes 1769480 | tf_op jit(solution)/shard_map/ppermute | solution.py:972
  197.5 20.2 %collective-permute-start.23 = (bf16[2,288,512]{2,1,0:T(8,128)(2,1)}, bf16[2,288,512]{2,1,0:T(8,128)(2,1)}, u32[]{:S(2)}, u32[]{:S(2)}) collective-permute-start(bf16[2,288,512]{2,1,0:T(8,128)(2,1)} %collective-permute-done.20.refs_5_), channel_id=1, source_target_pairs={{0,2},{2,0},{4,6},{6,4},{8,10},{10,8},{12,14},{14,12},{16,18},{18,... | collective-permute-start | bytes 1769480 | tf_op jit(solution)/shard_map/ppermute | solution.py:972
  210.9 19.0 %collective-permute-start.24 = (bf16[4,128,512]{2,1,0:T(8,128)(2,1)S(1)}, bf16[4,128,512]{2,1,0:T(8,128)(2,1)S(1)}, u32[]{:S(2)}, u32[]{:S(2)}) collective-permute-start(bf16[4,128,512]{2,1,0:T(8,128)(2,1)S(1)} %fusion.5), channel_id=1, source_target_pairs={{0,4},{2,6},{4,0},{6,2},{8,12},{10,14},{12,8},{14,10},{16,20},{18,... | collective-permute-start | bytes 1572872 | tf_op jit(solution)/shard_map/ppermute | solution.py:972
  212.4 20.8 %collective-permute-start.26 = (bf16[2,288,512]{2,1,0:T(8,128)(2,1)}, bf16[2,288,512]{2,1,0:T(8,128)(2,1)}, u32[]{:S(2)}, u32[]{:S(2)}) collective-permute-start(bf16[2,288,512]{2,1,0:T(8,128)(2,1)} %pad_maximum_fusion.2.refs_6_), channel_id=1, source_target_pairs={{0,2},{2,0},{4,6},{6,4},{8,10},{10,8},{12,14},{14,12},{16,18},{18,... | collective-permute-start | bytes 1769480 | tf_op jit(solution)/shard_map/ppermute | solution.py:972
  213.5 21.2 %collective-permute-start.27 = (bf16[2,288,512]{2,1,0:T(8,128)(2,1)}, bf16[2,288,512]{2,1,0:T(8,128)(2,1)}, u32[]{:S(2)}, u32[]{:S(2)}) collective-permute-start(bf16[2,288,512]{2,1,0:T(8,128)(2,1)} %collective-permute-done.25.refs_7_), channel_id=1, source_target_pairs={{0,2},{2,0},{4,6},{6,4},{8,10},{10,8},{12,14},{14,12},{16,18},{18,... | collective-permute-start | bytes 1769480 | tf_op jit(solution)/shard_map/ppermute | solution.py:972
  216.2 29.9 %collective-permute-start.31 = (bf16[2,4,112,512]{3,2,1,0:T(8,128)(2,1)S(1)}, bf16[2,4,112,512]{3,2,1,0:T(8,128)(2,1)}, u32[]{:S(2)}, u32[]{:S(2)}) collective-permute-start(bf16[2,4,112,512]{3,2,1,0:T(8,128)(2,1)S(1)} %fusion.2), channel_id=1, source_target_pairs={{0,1},{1,0},{2,3},{3,2},{4,5},{5,4},{6,7},{7,6},{8,9},{9,8},{10,11... | collective-permute-start | bytes 2752520 | tf_op jit(solution)/shard_map/ppermute | solution.py:976
  266.1 25.9 %collective-permute-start.47 = (bf16[4,128,512]{2,1,0:T(8,128)(2,1)S(1)}, bf16[4,128,512]{2,1,0:T(8,128)(2,1)S(1)}, u32[]{:S(2)}, u32[]{:S(2)}) collective-permute-start(bf16[4,128,512]{2,1,0:T(8,128)(2,1)S(1)} %pad_maximum_fusion.6.refs_1_), channel_id=1, source_target_pairs={{0,4},{2,6},{4,0},{6,2},{8,12},{10,14},{12,8},{14,10},{16,20},{18,... | collective-permute-start | bytes 1572872 | tf_op jit(solution)/shard_map/ppermute | solution.py:972
  294.2 16.2 %collective-permute-start.50 = (bf16[144,512]{1,0:T(8,128)(2,1)S(1)}, bf16[144,512]{1,0:T(8,128)(2,1)S(1)}, u32[]{:S(2)}, u32[]{:S(2)}) collective-permute-start(bf16[144,512]{1,0:T(8,128)(2,1)S(1)} %get-tuple-element.227), channel_id=1, source_target_pairs={{0,24},{2,26},{4,28},{6,30},{8,16},{10,18},{12,20},{14,22},{16,8},... | collective-permute-start | bytes 442376 | tf_op jit(solution)/shard_map/ppermute | solution.py:972
  294.7 21.5 %collective-permute-start.52 = (bf16[4,128,512]{2,1,0:T(8,128)(2,1)S(1)}, bf16[4,128,512]{2,1,0:T(8,128)(2,1)S(1)}, u32[]{:S(2)}, u32[]{:S(2)}) collective-permute-start(bf16[4,128,512]{2,1,0:T(8,128)(2,1)S(1)} %pad_maximum_fusion.6.refs_1_), channel_id=1, source_target_pairs={{0,2},{2,0},{4,6},{6,4},{8,10},{10,8},{12,14},{14,12},{16,18},{18,... | collective-permute-start | bytes 1572872 | tf_op jit(solution)/shard_map/ppermute | solution.py:972
  297.0 19.2 %collective-permute-start.53 = (bf16[4,128,512]{2,1,0:T(8,128)(2,1)S(1)}, bf16[4,128,512]{2,1,0:T(8,128)(2,1)S(1)}, u32[]{:S(2)}, u32[]{:S(2)}) collective-permute-start(bf16[4,128,512]{2,1,0:T(8,128)(2,1)S(1)} %collective-permute-done.47.refs_2_), channel_id=1, source_target_pairs={{0,2},{2,0},{4,6},{6,4},{8,10},{10,8},{12,14},{14,12},{16,18},{18,... | collective-permute-start | bytes 1572872 | tf_op jit(solution)/shard_map/ppermute | solution.py:972
  310.5 19.3 %collective-permute-start.51 = (bf16[4,144,512]{2,1,0:T(8,128)(2,1)S(1)}, bf16[4,144,512]{2,1,0:T(8,128)(2,1)S(1)}, u32[]{:S(2)}, u32[]{:S(2)}) collective-permute-start(bf16[4,144,512]{2,1,0:T(8,128)(2,1)S(1)} %pad_maximum_fusion.3.own_ref), channel_id=1, source_target_pairs={{0,4},{2,6},{4,0},{6,2},{8,12},{10,14},{12,8},{14,10},{16,20},{18,... | collective-permute-start | bytes 1769480 | tf_op jit(solution)/shard_map/ppermute | solution.py:972
  311.6 22.0 %collective-permute-start.32 = (bf16[2,128,512]{2,1,0:T(8,128)(2,1)S(1)}, bf16[2,128,512]{2,1,0:T(8,128)(2,1)S(1)}, u32[]{:S(2)}, u32[]{:S(2)}) collective-permute-start(bf16[2,128,512]{2,1,0:T(8,128)(2,1)S(1)} %get-tuple-element.214), channel_id=1, source_target_pairs={{0,0},{4,2},{8,4},{12,6},{16,8},{20,10},{24,12},{28,14},{30,16},{2... | collective-permute-start | bytes 786440 | tf_op jit(solution)/shard_map/ppermute | solution.py:1343
  313.5 20.1 %collective-permute-start.33 = (bf16[2,128,512]{2,1,0:T(8,128)(2,1)S(1)}, bf16[2,128,512]{2,1,0:T(8,128)(2,1)S(1)}, u32[]{:S(2)}, u32[]{:S(2)}) collective-permute-start(bf16[2,128,512]{2,1,0:T(8,128)(2,1)S(1)} %get-tuple-element.215), channel_id=1, source_target_pairs={{2,0},{6,2},{10,4},{14,6},{18,8},{22,10},{26,12},{30,14},{28,16},{... | collective-permute-start | bytes 786440 | tf_op jit(solution)/shard_map/ppermute | solution.py:1343
  (66 other events, 547.8 us)
Sparse Core Ops, SparseCore 0:
  10.9 53.2 all-gather.2
  256.5 65.1 reduce-scatter.1
